TPU v7x, 128 devices: a whole 4x4x4 slice. The times are simulated.
128 devices in a mesh: cfg: 2 (over z_lo), req: 8 (over z_hi, x), seq: 8 (over y, core).
Axes of the slice: x: 4, y: 4, z: 4 (z_hi: 2, z_lo: 2; z = z_hi * 2 + z_lo), core: 2. Of those that a mesh axis runs over, the one named last changes fastest.
Arguments:
- img_state: bfloat16 [2, 16, 1024, 1536], P('cfg', 'req', 'seq'), may hold values from -6 to 6
- txt_state: bfloat16 [2, 16, 192, 1536], P('cfg', 'req', 'seq'), may hold values from -6 to 6
- cond_vec: float32 [2, 16, 1536], P('cfg'), may hold values from -6 to 6
- text_len: int32 [2, 16], P('cfg', 'req'), may hold values from 38 to 154, as said below
- latent: float32 [16, 1024, 64], P('req', 'seq', 'cfg'), may hold values from -6 to 6
- w_mod: bfloat16 [15360, 1536], P(('req', 'seq')), may hold values from -0.15625 to 0.15625
- w_qkv_img: bfloat16 [3, 1536, 1536], P(None, 'seq')
- w_qkv_txt: bfloat16 [3, 1536, 1536], P(None, 'seq')
- w_attn_out: bfloat16 [1536, 1536], P('seq'), may hold values from -2 to 2
- w_up: bfloat16 [6144, 1536], P(('cfg', 'req', 'seq')), may hold values from -0.15625 to 0.15625
- w_down: bfloat16 [6144, 1536], P(('cfg', 'req', 'seq')), may hold values from -0.078125 to 0.078125
- w_final: bfloat16 [1536, 64], replicated, may hold values from -0.078125 to 0.078125
Outputs:
- velocity: float32 [16, 1024, 64], P('req', 'seq', 'cfg')
- latent_next: float32 [16, 1024, 64], P('req', 'seq', 'cfg')
Inputs may be any that keep to these rules, and one draw needn't show every extreme that they name: Text slot t of prompt p in branch c is live when t < text_len[c, p]; every draw has a length equal to 154.
All inputs are finite; a program needn't handle non-finite values.
Results may differ from a plain program's by a relative error of at most 0.02.
Values may be sent and summed in bfloat16 or wider, within the bound.
No kernel may reach another device: no remote copies, remote signals or barrier semaphores. Data moves between devices by JAX's collectives and lax.ppermute only.
A program may use at most 128 MiB of HBM per device.

v0:
```python
import jax
import jax.numpy as jnp
from jax import lax
from jax.sharding import PartitionSpec as P

HEAD = 64


def partner_2(shard, axis, apart):
    return lax.ppermute(shard, axis, [(i, i ^ 1 << apart) for i in range(lax.axis_size(axis))])


def layer_norm(value):
    mean = jnp.mean(value, axis=-1, keepdims=True)
    centered = value - mean
    spread = jnp.mean(centered * centered, axis=-1, keepdims=True)
    return centered * lax.rsqrt(spread + 1e-06)


def mlp_term(rows_in, up_block, down_block):
    inner = lax.dot_general(
        rows_in, up_block, (((1,), (1,)), ((), ())), preferred_element_type=jnp.float32
    )
    hidden = jax.nn.gelu(inner, approximate=True).astype(jnp.bfloat16)
    return jnp.dot(hidden, down_block, preferred_element_type=jnp.float32)


def local(
    img_state,
    txt_state,
    cond_vec,
    text_len,
    latent,
    w_mod,
    w_qkv_img,
    w_qkv_txt,
    w_attn_out,
    w_up,
    w_down,
    w_final,
):
    prompts_dev = img_state.shape[1]
    img_rows = img_state.shape[2]
    width = img_state.shape[3]
    cond_act = jax.nn.silu(cond_vec[0]).astype(jnp.bfloat16)
    mod_part = lax.dot_general(
        cond_act, w_mod, (((1,), (1,)), ((), ())), preferred_element_type=jnp.float32
    )
    mod_all = lax.all_gather(mod_part, ("req", "seq"), axis=1, tiled=True)
    mine = lax.dynamic_slice_in_dim(mod_all, lax.axis_index("req") * prompts_dev, prompts_dev, 0)
    parts = mine.reshape(prompts_dev, 10, 1, width)
    resid = img_state[0].astype(jnp.float32)
    a_img = (layer_norm(resid) * (1.0 + parts[:, 1]) + parts[:, 0]).astype(jnp.bfloat16)
    a_txt = (
        layer_norm(txt_state[0].astype(jnp.float32)) * (1.0 + parts[:, 7]) + parts[:, 6]
    ).astype(jnp.bfloat16)
    full_img, full_txt = (
        lax.all_gather(a_img, "seq", axis=1, tiled=True),
        lax.all_gather(a_txt, "seq", axis=1, tiled=True),
    )
    proj_img = jnp.einsum(
        "pnd,jed->jpne", full_img, w_qkv_img, preferred_element_type=jnp.float32
    ).astype(jnp.bfloat16)
    proj_txt = jnp.einsum(
        "pnd,jed->jpne", full_txt, w_qkv_txt, preferred_element_type=jnp.float32
    ).astype(jnp.bfloat16)
    total_img = full_img.shape[1]
    local_width = w_qkv_img.shape[1]
    heads_local = local_width // HEAD
    key_heads = jnp.concatenate([proj_img[1], proj_txt[1]], axis=1).reshape(
        prompts_dev, -1, heads_local, HEAD
    )
    value_heads = jnp.concatenate([proj_img[2], proj_txt[2]], axis=1).reshape(
        prompts_dev, -1, heads_local, HEAD
    )
    live = jnp.arange(key_heads.shape[1])[None, :] < (total_img + text_len[0])[:, None]
    block = min(512, total_img)
    queries = proj_img[0].reshape(prompts_dev, total_img // block, block, heads_local, HEAD)

    def attend(query):
        scores = jnp.einsum(
            "pqhe,pkhe->phqk", query, key_heads, preferred_element_type=jnp.float32
        ) * HEAD ** (-0.5)
        scores = jnp.where(live[:, None, None, :], scores, -1e30)
        probs = jax.nn.softmax(scores, axis=-1).astype(jnp.bfloat16)
        return jnp.einsum(
            "phqk,pkhe->pqhe", probs, value_heads, preferred_element_type=jnp.float32
        ).astype(jnp.bfloat16)

    attended = lax.map(attend, jnp.moveaxis(queries, 1, 0))
    attended = jnp.moveaxis(attended, 0, 1).reshape(prompts_dev, total_img, local_width)
    proj = jnp.swapaxes(
        lax.psum_scatter(
            jnp.einsum(
                "pnh,hd->npd", attended, w_attn_out, preferred_element_type=jnp.float32
            ).astype(jnp.bfloat16),
            "seq",
            scatter_dimension=0,
            tiled=True,
        ).astype(jnp.float32),
        0,
        1,
    )
    resid_one = (resid + parts[:, 2] * proj).astype(jnp.bfloat16)
    normed = (layer_norm(resid_one.astype(jnp.float32)) * (1.0 + parts[:, 4]) + parts[:, 3]).astype(
        jnp.bfloat16
    )
    own_rows = normed.reshape(prompts_dev * img_rows, width)
    both = lax.all_gather(own_rows, "cfg", axis=0, tiled=True)
    partial_out = mlp_term(
        both,
        lax.all_gather(w_up, ("req", "seq"), axis=0, tiled=True),
        lax.all_gather(w_down, ("req", "seq"), axis=0, tiled=True),
    )
    mlp_out = lax.psum_scatter(
        partial_out.astype(jnp.bfloat16), "cfg", scatter_dimension=0, tiled=True
    ).astype(jnp.float32)
    mlp_out = mlp_out.reshape(prompts_dev, img_rows, width)
    resid_two = resid_one.astype(jnp.float32) + parts[:, 5] * mlp_out
    final_in = (layer_norm(resid_two) * (1.0 + parts[:, 9]) + parts[:, 8]).astype(jnp.bfloat16)
    branch_vel = jnp.einsum("pnd,dc->pnc", final_in, w_final, preferred_element_type=jnp.float32)
    half_width = latent.shape[2]
    branch_index = lax.axis_index("cfg")
    own_half = lax.dynamic_slice_in_dim(branch_vel, branch_index * half_width, half_width, 2)
    other_half = lax.dynamic_slice_in_dim(
        branch_vel, (1 - branch_index) * half_width, half_width, 2
    )
    partner = partner_2(other_half.astype(jnp.bfloat16), "cfg", 0).astype(other_half.dtype)
    first = branch_index == 0
    cond_vel = jnp.where(first, own_half, partner)
    uncond_vel = jnp.where(first, partner, own_half)
    velocity = uncond_vel + 4.5 * (cond_vel - uncond_vel)
    latent_next = latent - 0.04 * velocity
    return (velocity, latent_next)


def solution(mesh):
    placed = (
        P("cfg", "req", "seq", None),
        P("cfg", "req", "seq", None),
        P("cfg", None, None),
        P("cfg", "req"),
        P("req", "seq", "cfg"),
        P(("req", "seq"), None),
        P(None, "seq", None),
        P(None, "seq", None),
        P("seq", None),
        P(("cfg", "req", "seq"), None),
        P(("cfg", "req", "seq"), None),
        P(),
    )
    return jax.shard_map(
        local,
        mesh=mesh,
        in_specs=placed,
        out_specs=(P("req", "seq", "cfg"), P("req", "seq", "cfg")),
        check_vma=False,
    )
```

profile of v0, /device:TPU:70, one launch (start us, length us, event | category | flops | bytes accessed | tf_op | source)
XLA Modules:
  0.0 503.2 jit_solution(12453538248403719071)
XLA Ops:
  8.1 1.6 convolution_bitcast_fusion
  9.6 84.0 %all-gather = f32[64,240,16]{1,2,0:T(8,128)S(1)} all-gather(f32[1,240,16]{1,2,0:T(8,128)S(1)} %convolution_bitcast_fusion), channel_id=1, replica_groups=mesh['cfg'=2,'req'=8,'seq'=8] {'req','seq'}, dimensions={0}, use_global_device_ids=true | all-gather | bytes 998400 | tf_op jit(solution)/shard_map/all_gather | solution.py:49
  93.6 1.6 copy.18
  95.2 2.9 reshape.139
  103.2 30.7 %all-gather.9.cloned.1.call-done = bf16[2,192,1536]{2,1,0:T(8,128)(2,1)} async-done(((bf16[2,24,1536]{2,1,0:T(8,128)(2,1)}), bf16[2,192,1536]{2,1,0:T(8,128)(2,1)}) %all-gather.9.cloned.1.call-update) | async-done | bytes 1179664 | tf_op jit(solution)/shard_map/all_gather | solution.py:59
  133.9 2.9 fusion.83
  137.7 39.0 %all-gather.7.cloned.1.call-done = bf16[2,1024,1536]{2,1,0:T(8,128)(2,1)} async-done(((bf16[2,128,1536]{2,1,0:T(8,128)(2,1)}), bf16[2,1024,1536]{2,1,0:T(8,128)(2,1)}) %all-gather.7.cloned.1.call-update) | async-done | bytes 6291472 | tf_op jit(solution)/shard_map/all_gather | solution.py:58
  176.6 6.8 %convert_bitcast_fusion.1 = bf16[3,2,1024,192]{2,3,0,1:T(8,128)(2,1)S(1)} fusion(bf16[2,1024,1536]{2,1,0:T(8,128)(2,1)} %all-gather.7.cloned.1.call-done, bf16[3,192,1536]{2,1,0:T(8,128)(2,1)S(1)} %copy-done), kind=kOutput, calls=%fused_computation.51 | convolution fusion | flops 3625058304 | bytes 10420224 | tf_op jit(solution)/shard_map/pnd,jed->jpne/dot_general | solution.py:61
  186.4 2.3 copy.44
  190.8 31.2 %while.11 = (s32[]{:T(128)}, bf16[2,2,512,3,64]{2,4,3,1,0:T(8,128)(2,1)}, bf16[2,2,512,3,64]{2,4,3,1,0:T(8,128)(2,1)}, bf16[2,1216,3,64]{1,3,2,0:T(8,128)(2,1)},...) while((s32[]{:T(128)}, bf16[2,2,512,3,64]{2,4,3,1,0:T(8,128)(2,1)}, ...), condition=%wide.region_7.8_spmd.clone, body=%wide.region_4.7_spmd.clone.sunk | while | flops 1468276480 | bytes 4117205 | solution.py:90
  190.8 7.2 %fusion.142 = f32[2,3,512]{2,1,0:T(4,128)} fusion(pred[2,1216]{1,0:T(4,128)(4,1)S(1)} %iota_compare_fusion.2, bf16[2,1216,3,64]{1,3,2,0:T(8,128)(2,1)} %get-tuple-element.143, bf16[2,2,512,3,64]{2,4,3,1,0:T(8,128)(2,1)} %get-tuple-element.142, s32[]{:T(128)} %get-tuple-element.133), kind=kOutput, calls=%fused_computation.138.clone.1 | convolution fusion | flops 493094080 | bytes 1391488 | tf_op jit(solution)/shard_map/while/body/eval_jaxpr/sub | solution.py:85
  198.0 8.3 %fusion.143 = bf16[2,2,512,3,64]{2,4,3,1,0:T(8,128)(2,1)} fusion(bf16[2,2,512,3,64]{2,4,3,1,0:T(8,128)(2,1)} %get-tuple-element.134, s32[]{:T(128)} %get-tuple-element.133, bf16[2,1216,3,64]{1,3,2,0:T(8,128)(2,1)S(1)} %get-tuple-element.144, f32[2,3,512]{2,1,0:T(4,128)} %fusion.142, pred[2,1216]{1,0:T(4,128)(4,1)S(1)} %iota_compare_fusion.2, ...), kind=kOutput, calls=%fused_computation.13.clone.1 | convolution fusion | flops 975179968 | bytes 2723200 | tf_op jit(solution)/shard_map/while/body/eval_jaxpr/phqk,pkhe->pqhe/dot_general | solution.py:86
  206.4 7.2 %fusion.142 = f32[2,3,512]{2,1,0:T(4,128)} fusion(pred[2,1216]{1,0:T(4,128)(4,1)S(1)} %iota_compare_fusion.2, bf16[2,1216,3,64]{1,3,2,0:T(8,128)(2,1)} %get-tuple-element.143, bf16[2,2,512,3,64]{2,4,3,1,0:T(8,128)(2,1)} %get-tuple-element.142, s32[]{:T(128)} %get-tuple-element.133), kind=kOutput, calls=%fused_computation.138.clone.1 | convolution fusion | flops 493094080 | bytes 1391488 | tf_op jit(solution)/shard_map/while/body/eval_jaxpr/sub | solution.py:85
  213.6 8.3 %fusion.143 = bf16[2,2,512,3,64]{2,4,3,1,0:T(8,128)(2,1)} fusion(bf16[2,2,512,3,64]{2,4,3,1,0:T(8,128)(2,1)} %get-tuple-element.134, s32[]{:T(128)} %get-tuple-element.133, bf16[2,1216,3,64]{1,3,2,0:T(8,128)(2,1)S(1)} %get-tuple-element.144, f32[2,3,512]{2,1,0:T(4,128)} %fusion.142, pred[2,1216]{1,0:T(4,128)(4,1)S(1)} %iota_compare_fusion.2, ...), kind=kOutput, calls=%fused_computation.13.clone.1 | convolution fusion | flops 975179968 | bytes 2723200 | tf_op jit(solution)/shard_map/while/body/eval_jaxpr/phqk,pkhe->pqhe/dot_general | solution.py:86
  222.0 2.8 copy.20
  224.8 2.5 reshape.132
  227.3 5.5 %convert_bitcast_fusion = bf16[1024,2,1536]{2,0,1:T(8,128)(2,1)} fusion(bf16[2,1024,192]{1,2,0:T(8,128)(2,1)S(1)} %reshape.132, bf16[192,1536]{1,0:T(8,128)(2,1)} %param.22), kind=kOutput, calls=%fused_computation.41 | convolution fusion | flops 1211105280 | bytes 7667712 | tf_op jit(solution)/shard_map/pnh,hd->npd/dot_general | solution.py:94
  234.1 43.4 %reduce-scatter.3.cloned.1.call-done = bf16[128,2,1536]{2,0,1:T(8,128)(2,1)} async-done(((bf16[1024,2,1536]{2,0,1:T(8,128)(2,1)}), bf16[128,2,1536]{2,0,1:T(8,128)(2,1)}) %reduce-scatter.3.cloned.1.call-update) | async-done | bytes 786448 | tf_op jit(solution)/shard_map/reduce_scatter | solution.py:93
  280.8 42.3 %all-gather.13.cloned.1.call-done = bf16[3072,1536]{1,0:T(8,128)(2,1)} async-done(((bf16[48,1536]{1,0:T(8,128)(2,1)}), bf16[3072,1536]{1,0:T(8,128)(2,1)}) %all-gather.13.cloned.1.call-update) | async-done | bytes 9437200 | tf_op jit(solution)/shard_map/all_gather | solution.py:112
  323.1 86.0 %all-gather.15.cloned.1.call-done = bf16[3072,1536]{1,0:T(8,128)(2,1)} async-done(((bf16[48,1536]{1,0:T(8,128)(2,1)}), bf16[3072,1536]{1,0:T(8,128)(2,1)}) %all-gather.15.cloned.1.call-update) | async-done | bytes 9437200 | tf_op jit(solution)/shard_map/all_gather | solution.py:113
  409.0 32.0 %all-gather.11.cloned.1.call-done = bf16[512,1536]{1,0:T(8,128)(2,1)} async-done(((bf16[256,1536]{1,0:T(8,128)(2,1)}), bf16[512,1536]{1,0:T(8,128)(2,1)}) %all-gather.11.cloned.1.call-update) | async-done | bytes 1572880 | tf_op jit(solution)/shard_map/all_gather | solution.py:109
  441.1 18.0 %fusion.57 = bf16[512,1536]{1,0:T(8,128)(2,1)} fusion(bf16[3072,1536]{1,0:T(8,128)(2,1)} %all-gather.15.cloned.1.call-done, bf16[512,1536]{1,0:T(8,128)(2,1)} %all-gather.11.cloned.1.call-done, bf16[3072,1536]{1,0:T(8,128)(2,1)} %all-gather.13.cloned.1.call-done), kind=kOutput, calls=%fused_computation.47 | convolution fusion | flops 9678618624 | bytes 22020096 | tf_op jit(solution)/shard_map/dot_general | solution.py:25
  459.2 29.6 %reduce-scatter.5.cloned.1.call-done = bf16[256,1536]{1,0:T(8,128)(2,1)} async-done(((bf16[512,1536]{1,0:T(8,128)(2,1)}), bf16[256,1536]{1,0:T(8,128)(2,1)}) %reduce-scatter.5.cloned.1.call-update) | async-done | bytes 786448 | tf_op jit(solution)/shard_map/reduce_scatter | solution.py:115
  492.2 3.0 collective-permute-done
  (87 shorter events, 19.5 us)
Async XLA Ops:
  8.0 168.7 %copy-start = (bf16[3,192,1536]{2,1,0:T(8,128)(2,1)S(1)}, bf16[3,192,1536]{2,1,0:T(8,128)(2,1)}, u32[]{:S(2)}) copy-start(bf16[3,192,1536]{2,1,0:T(8,128)(2,1)} %param.20) | copy-start | bytes 5308420
  8.0 125.9 %all-gather.9.cloned.1.call-start = ((), (), s32[]{:S(2)}) async-start(), calls=%async_computation.3 | async-start | bytes 1327104 | tf_op jit(solution)/shard_map/all_gather | solution.py:59
  95.2 4.8 copy-start.5
  95.2 6.0 %copy-start.1 = (bf16[1,2,128,1536]{3,2,1,0:T(8,128)(2,1)S(1)}, bf16[1,2,128,1536]{3,2,1,0:T(8,128)(2,1)}, u32[]{:S(2)}) copy-start(bf16[1,2,128,1536]{3,2,1,0:T(8,128)(2,1)} %param.14) | copy-start | bytes 2359300
  101.2 75.5 %all-gather.7.cloned.1.call-start = ((), (), s32[]{:S(2)}) async-start(), calls=%async_computation.2 | async-start | bytes 7077888 | tf_op jit(solution)/shard_map/all_gather | solution.py:58
  101.4 1.8 copy-start.15
  103.2 174.4 %reduce-scatter.3.cloned.1.call-start = ((), (), s32[]{:S(2)}) async-start(), calls=%async_computation.4 | async-start | bytes 7077888 | tf_op jit(solution)/shard_map/reduce_scatter | solution.py:93
  186.4 2.3 copy-start.3
  186.4 3.3 copy-start.2
  186.4 3.3 copy-start.6
  232.8 1.2 copy-start.8
  232.8 1.3 copy-start.11
  232.8 1.3 copy-start.12
  232.8 90.2 %all-gather.13.cloned.1.call-start = ((), (), s32[]{:S(2)}) async-start(), calls=%async_computation.6 | async-start | bytes 9584640 | tf_op jit(solution)/shard_map/all_gather | solution.py:112
  233.4 175.6 %all-gather.15.cloned.1.call-start = ((), (), s32[]{:S(2)}) async-start(), calls=%async_computation.7 | async-start | bytes 9584640 | tf_op jit(solution)/shard_map/all_gather | solution.py:113
  234.0 207.0 %all-gather.11.cloned.1.call-start = ((), (), s32[]{:S(2)}) async-start(), calls=%async_computation.5 | async-start | bytes 2359296 | tf_op jit(solution)/shard_map/all_gather | solution.py:109
  280.7 178.4 %copy-start.7 = (f32[2,1,1,1536]{3,1,0,2:T(1,128)S(1)}, f32[2,1,1,1536]{3,1,0,2:T(1,128)}, u32[]{:S(2)}) copy-start(f32[2,1,1,1536]{3,1,0,2:T(1,128)} %get-tuple-element.71) | copy-start | bytes 36868
  280.7 178.4 %copy-start.9 = (f32[2,1,1,1536]{3,1,0,2:T(1,128)S(1)}, f32[2,1,1,1536]{3,1,0,2:T(1,128)}, u32[]{:S(2)}) copy-start(f32[2,1,1,1536]{3,1,0,2:T(1,128)} %get-tuple-element.72) | copy-start | bytes 36868
  280.7 178.4 %copy-start.10 = (f32[2,1,1,1536]{3,1,0,2:T(1,128)S(1)}, f32[2,1,1,1536]{3,1,0,2:T(1,128)}, u32[]{:S(2)}) copy-start(f32[2,1,1,1536]{3,1,0,2:T(1,128)} %get-tuple-element.73) | copy-start | bytes 36868
  280.7 208.0 %reduce-scatter.5.cloned.1.call-start = ((), (), s32[]{:S(2)}) async-start(), calls=%async_computation.8 | async-start | bytes 2359296 | tf_op jit(solution)/shard_map/reduce_scatter | solution.py:115
  459.1 31.7 %copy-start.14 = (bf16[1536,64]{0,1:T(8,128)(2,1)S(1)}, bf16[1536,64]{0,1:T(8,128)(2,1)}, u32[]{:S(2)}) copy-start(bf16[1536,64]{0,1:T(8,128)(2,1)} %param.25) | copy-start | bytes 589828
  488.7 1.6 copy-start.4
  490.7 4.5 copy-start.13
  491.4 3.8 collective-permute-start
Sparse Core Ops, SparseCore 0:
  101.3 32.5 all-gather.8
  135.6 40.9 all-gather.6
  233.0 44.5 reduce-scatter.2
Sparse Core Ops, SparseCore 1:
  236.4 86.6 all-gather.12
  326.0 82.9 all-gather.14
  410.5 30.5 all-gather.10
  459.2 29.5 reduce-scatter.4
where the time goes:
time: 505 us; the launch traced here: 503 us
  waiting for transfers between devices  307 us (61%)
  blocking collectives  84 us (17%)
  matrix products  66.5 us (13%)
  local copies, waits for them, and re-layouts  17.2 us (3%)
  between operations  15.8 us (3%)
  other arithmetic  11.6 us (2%)
    all_gather x1, waiting for transfers between devices, local(): lax.all_gather(w_down, ('req', 'seq'), axis=0, tiled=True)  86 us
    all_gather x1, blocking collectives, local(): mod_all = lax.all_gather(mod_part, ('req', 'seq'), axis=1, tiled=True)  84 us
    reduce_scatter x1, waiting for transfers between devices, local(): lax.psum_scatter(jnp.einsum('pnh,hd->npd', attended, w_attn_out, preferre...  43.4 us
    all_gather x1, waiting for transfers between devices, local(): lax.all_gather(w_up, ('req', 'seq'), axis=0, tiled=True)  42.3 us
    all_gather x1, waiting for transfers between devices, local(): lax.all_gather(a_img, 'seq', axis=1, tiled=True)  39 us
    all_gather x1, waiting for transfers between devices, local(): both = lax.all_gather(own_rows, 'cfg', axis=0, tiled=True)  32 us
    all_gather x1, waiting for transfers between devices, local(): lax.all_gather(a_txt, 'seq', axis=1, tiled=True)  30.7 us
    reduce_scatter x1, waiting for transfers between devices, local(): lax.psum_scatter(partial_out.astype(jnp.bfloat16), 'cfg', scatter_dimensi...  29.6 us
  transfers between devices with their start and end apart: 8, of which 8 were waited for; matrix products, arithmetic and copies ran while one was open for 2% of the time, Pallas kernels for 0%

commit v1 on v0

v1 whole, which is shorter than its diff:
```python
import math

import jax
import jax.numpy as jnp
import numpy as np
from jax import lax
from jax.experimental import pallas as pl
from jax.experimental.pallas import tpu as pltpu
from jax.sharding import Mesh
from jax.sharding import PartitionSpec as P

HEAD = 64
SEQ = ("y", "core")
REQ = ("zhi", "x")
NT = (((1,), (1,)), ((), ()))
NN = (((1,), (0,)), ((), ()))
TXT_PAD = 32


def dot(a, b, dims):
    return lax.dot_general(a, b, dims, preferred_element_type=jnp.float32)


def layer_norm(value):
    mean = jnp.mean(value, axis=-1, keepdims=True)
    centered = value - mean
    spread = jnp.mean(centered * centered, axis=-1, keepdims=True)
    return centered * lax.rsqrt(spread + 1e-06)


def attn_kernel(seqs, rows, txt, x_ref, mod_ref, bias_ref, wi_ref, wt_ref, out_ref, ai, at, k_s, v_s, q_s):
    block = rows + TXT_PAD
    img = seqs * rows
    keys = seqs * block
    for s in range(seqs):
        part = x_ref[0, s * block : s * block + rows, :].astype(jnp.float32)
        normed = layer_norm(part) * (1.0 + mod_ref[0, 1:2, :]) + mod_ref[0, 0:1, :]
        ai[s * rows : (s + 1) * rows, :] = normed.astype(jnp.bfloat16)
        part = x_ref[0, s * block + rows : (s + 1) * block, :].astype(jnp.float32)
        normed = layer_norm(part) * (1.0 + mod_ref[0, 7:8, :]) + mod_ref[0, 6:7, :]
        at[s * TXT_PAD : (s + 1) * TXT_PAD, :] = normed.astype(jnp.bfloat16)
    width = wi_ref.shape[1]
    heads = width // HEAD
    a_img, a_txt = ai[...], at[...]
    k_s[0:img, :] = dot(a_img, wi_ref[1], NT).astype(jnp.bfloat16)
    k_s[img:keys, :] = dot(a_txt, wt_ref[1], NT).astype(jnp.bfloat16)
    q_s[...] = (dot(wi_ref[0], a_img, NT) * (HEAD ** (-0.5) * math.log2(math.e))).astype(jnp.bfloat16)
    v_img = dot(wi_ref[2], a_img, NT).astype(jnp.bfloat16)
    v_txt = dot(wt_ref[2], a_txt, NT).astype(jnp.bfloat16)
    ones = jnp.ones((16, keys), jnp.bfloat16)
    for h in range(heads):
        v_s[h, 0:HEAD, 0:img] = v_img[h * HEAD : (h + 1) * HEAD, :]
        v_s[h, 0:HEAD, img:keys] = v_txt[h * HEAD : (h + 1) * HEAD, :]
        v_s[h, HEAD : HEAD + 16, :] = ones
    step = 256
    k_all = k_s[...]
    bias = bias_ref[0]
    for h in range(heads):
        for c in range(img // step):
            q_h = q_s[h * HEAD : (h + 1) * HEAD, c * step : (c + 1) * step]
            pieces = []
            if h:
                pieces.append(jnp.zeros((h * HEAD, step), jnp.bfloat16))
            pieces.append(q_h)
            if h + 1 < heads:
                pieces.append(jnp.zeros(((heads - 1 - h) * HEAD, step), jnp.bfloat16))
            q_h = jnp.concatenate(pieces, axis=0) if len(pieces) > 1 else q_h
            s_img = dot(k_all[0:img], q_h, NN)
            s_txt = dot(k_all[img:keys], q_h, NN) + bias
            top = jnp.maximum(
                jnp.max(s_img, axis=0, keepdims=True), jnp.max(s_txt, axis=0, keepdims=True)
            )
            p_img = jnp.exp2(s_img - top).astype(jnp.bfloat16)
            p_txt = jnp.exp2(s_txt - top).astype(jnp.bfloat16)
            o = dot(v_s[h, :, 0:img], p_img, NN) + dot(v_s[h, :, img:keys], p_txt, NN)
            o = (o[0:HEAD] / o[HEAD : HEAD + 1]).astype(jnp.bfloat16)
            for i in range(step // rows):
                out_ref[c * (step // rows) + i, h * HEAD : (h + 1) * HEAD, :] = o[
                    :, i * rows : (i + 1) * rows
                ]


def attention(prompt, tokens, mod, bias, w_img, w_txt, seqs, rows):
    block = rows + TXT_PAD
    keys = seqs * block
    width = w_img.shape[1]
    depth = w_img.shape[2]
    heads = width // HEAD
    return pl.pallas_call(
        lambda *refs: attn_kernel(seqs, rows, TXT_PAD, *refs),
        out_shape=jax.ShapeDtypeStruct((seqs, width, rows), jnp.bfloat16),
        grid=(1,),
        in_specs=[
            pl.BlockSpec((1, keys, depth), lambda i: (prompt, 0, 0)),
            pl.BlockSpec((1, 10, depth), lambda i: (prompt, 0, 0)),
            pl.BlockSpec((1, seqs * TXT_PAD, 1), lambda i: (prompt, 0, 0)),
            pl.BlockSpec(w_img.shape, lambda i: (0, 0, 0)),
            pl.BlockSpec(w_txt.shape, lambda i: (0, 0, 0)),
        ],
        out_specs=pl.BlockSpec((seqs, width, rows), lambda i: (0, 0, 0)),
        scratch_shapes=[
            pltpu.VMEM((seqs * rows, depth), jnp.bfloat16),
            pltpu.VMEM((seqs * TXT_PAD, depth), jnp.bfloat16),
            pltpu.VMEM((keys, width), jnp.bfloat16),
            pltpu.VMEM((heads, HEAD + 16, keys), jnp.bfloat16),
            pltpu.VMEM((width, seqs * rows), jnp.bfloat16),
        ],
        compiler_params=pltpu.CompilerParams(vmem_limit_bytes=48 << 20),
        cost_estimate=pl.CostEstimate(flops=1000000, bytes_accessed=1000000, transcendentals=0),
        name="attn",
    )(tokens, mod, bias, w_img, w_txt)


def mlp_kernel(x_ref, up_ref, down_ref, out_ref, acc):
    step = pl.program_id(0)
    depth = up_ref.shape[-1]
    up = up_ref[...].reshape(-1, depth)
    down = down_ref[...].reshape(-1, depth)
    hidden = jax.nn.gelu(dot(x_ref[...], up, NT), approximate=True).astype(jnp.bfloat16)
    term = dot(hidden, down, NN)

    @pl.when(step == 0)
    def _():
        acc[...] = term

    @pl.when(step > 0)
    def _():
        acc[...] += term

    @pl.when(step == pl.num_programs(0) - 1)
    def _():
        out_ref[...] = acc[...].astype(out_ref.dtype)


def mlp(rows_in, weights, out_type):
    shards, _, units, width = weights.shape
    many = 8
    count = rows_in.shape[0]
    return pl.pallas_call(
        mlp_kernel,
        out_shape=jax.ShapeDtypeStruct((count, width), out_type),
        grid=(shards // many,),
        in_specs=[
            pl.BlockSpec((count, width), lambda i: (0, 0)),
            pl.BlockSpec((many, 1, units, width), lambda i: (i, 0, 0, 0)),
            pl.BlockSpec((many, 1, units, width), lambda i: (i, 1, 0, 0)),
        ],
        out_specs=pl.BlockSpec((count, width), lambda i: (0, 0)),
        scratch_shapes=[pltpu.VMEM((count, width), jnp.float32)],
        compiler_params=pltpu.CompilerParams(vmem_limit_bytes=40 << 20),
        cost_estimate=pl.CostEstimate(
            flops=4 * count * shards * units * width,
            bytes_accessed=4 * shards * units * width,
            transcendentals=0,
        ),
        name="mlp",
    )(rows_in, weights, weights)


def swap_cfg(value):
    return lax.ppermute(value, "cfg", [(0, 1), (1, 0)])


def local(
    img_state,
    txt_state,
    cond_vec,
    text_len,
    latent,
    w_mod,
    w_qkv_img,
    w_qkv_txt,
    w_attn_out,
    w_up,
    w_down,
    w_final,
):
    prompts = img_state.shape[1]
    rows = img_state.shape[2]
    width = img_state.shape[3]
    txt_rows = txt_state.shape[2]
    seqs = lax.axis_size("y") * lax.axis_size("core")
    reqs = lax.axis_size("zhi") * lax.axis_size("x")
    everyone = reqs * seqs

    padding = jnp.zeros((prompts, TXT_PAD - txt_rows, width), jnp.bfloat16)
    mine = jnp.concatenate([img_state[0], txt_state[0], padding], axis=1)
    tokens = lax.all_gather(mine, SEQ, axis=1, tiled=True)

    cond_act = jax.nn.silu(cond_vec[0]).astype(jnp.bfloat16)
    part = dot(cond_act, w_mod, NT)
    cols = part.shape[1]
    lanes = -(-cols // 128) * 128
    part = jnp.pad(part, ((0, 0), (0, lanes - cols)))
    part = part.reshape(reqs, 1, prompts * lanes // 128, 128)
    part = jnp.broadcast_to(part, (reqs, seqs) + part.shape[2:]).reshape((everyone,) + part.shape[2:])
    got = lax.all_to_all(part, REQ + SEQ, 0, 0, tiled=True)
    got = got.reshape(everyone, prompts, lanes)[:, :, :cols]
    mod = jnp.swapaxes(got, 0, 1).reshape(prompts, 10, width)

    w_out = lax.all_gather(w_attn_out, SEQ, axis=0, tiled=True)
    weights = lax.all_gather(jnp.stack([w_up, w_down])[None], REQ + SEQ, axis=0, tiled=True)

    slot = jnp.arange(seqs * TXT_PAD)
    inside = slot % TXT_PAD
    index = slot // TXT_PAD * txt_rows + inside
    live = (inside < txt_rows)[None, :] & (index[None, :] < text_len[0][:, None])
    bias = jnp.where(live, 0.0, -1e30).astype(jnp.float32)[:, :, None]

    normed, resid = [], []
    for p in range(prompts):
        att = attention(p, tokens, mod, bias, w_qkv_img, w_qkv_txt, seqs, rows)
        att = lax.all_to_all(att, SEQ, 0, 0, tiled=True).reshape(-1, rows)
        proj = dot(att, w_out, (((0,), (0,)), ((), ())))
        one = (img_state[0, p].astype(jnp.float32) + mod[p, 2] * proj).astype(jnp.bfloat16)
        resid.append(one)
        normed.append(
            (layer_norm(one.astype(jnp.float32)) * (1.0 + mod[p, 4]) + mod[p, 3]).astype(
                jnp.bfloat16
            )
        )
    other = [swap_cfg(n) for n in normed]
    for_other = mlp(jnp.concatenate(other, axis=0), weights, jnp.bfloat16)
    back = swap_cfg(for_other)
    own = mlp(jnp.concatenate(normed, axis=0), weights, jnp.float32)
    mlp_out = (own + back.astype(jnp.float32)).reshape(prompts, rows, width)
    resid_two = jnp.stack(resid).astype(jnp.float32) + mod[:, 5:6] * mlp_out
    final_in = (layer_norm(resid_two) * (1.0 + mod[:, 9:10]) + mod[:, 8:9]).astype(jnp.bfloat16)
    branch_vel = dot(final_in.reshape(prompts * rows, width), w_final, NN)
    branch_vel = branch_vel.reshape(prompts, rows, -1)
    half = latent.shape[2]
    branch = lax.axis_index("cfg")
    first = branch == 0
    low, high = branch_vel[:, :, :half], branch_vel[:, :, half:]
    own_half = jnp.where(first, low, high)
    partner = swap_cfg(jnp.where(first, high, low).astype(jnp.bfloat16)).astype(jnp.float32)
    cond_vel = jnp.where(first, own_half, partner)
    uncond_vel = jnp.where(first, partner, own_half)
    velocity = uncond_vel + 4.5 * (cond_vel - uncond_vel)
    return velocity, latent - 0.04 * velocity


def solution(mesh):
    fine = Mesh(np.asarray(mesh.devices).reshape(2, 2, 4, 4, 2), ("cfg", "zhi", "x", "y", "core"))
    every = ("cfg",) + REQ + SEQ
    placed = (
        P("cfg", REQ, SEQ, None),
        P("cfg", REQ, SEQ, None),
        P("cfg", None, None),
        P("cfg", REQ),
        P(REQ, SEQ, "cfg"),
        P(REQ + SEQ, None),
        P(None, SEQ, None),
        P(None, SEQ, None),
        P(SEQ, None),
        P(every, None),
        P(every, None),
        P(),
    )
    return jax.shard_map(
        local,
        mesh=fine,
        in_specs=placed,
        out_specs=(P(REQ, SEQ, "cfg"), P(REQ, SEQ, "cfg")),
        check_vma=False,
    )
```

time: 505 us -> 266 us (0.53)
  waiting for transfers between devices: 307 us -> 143 us
  blocking collectives: 84 us -> 0 us
  Pallas kernels: 0 us -> 59.8 us
  matrix products: 66.5 us -> 7.43 us
  starting transfers between devices: 1.13 us -> 25.7 us
  local copies, waits for them, and re-layouts: 17.2 us -> 4.63 us
    all_gather x5 -> x3, waiting for transfers between devices: 230 us -> 115 us  [the longest x1 83.7 us: local(): lax.all_gather(jnp.stack([w_up, w_down])[None], REQ + SEQ, axis=0, tiled=...]
    all_gather x1 -> x0, blocking collectives: 84 us -> none  [local(): mod_all = lax.all_gather(mod_part, ('req', 'seq'), axis=1, tiled=True)]
    reduce_scatter x2 -> x0, waiting for transfers between devices: 73 us -> none  [the longest x1 43.4 us: local(): lax.psum_scatter(jnp.einsum('pnh,hd->npd', attended, w_attn_out, preferre...]
    pallas_call x0 -> x4, Pallas kernels: none -> 59.8 us  [the longest x2 33.3 us: attention(): pl.pallas_call(lambda *refs: attn_kernel(seqs, rows, TXT_PAD, *refs), out...]
    dot_general x8 -> x4, matrix products: 52 us -> 7.43 us  [dot(): return lax.dot_general(a, b, dims, preferred_element_type=jnp.float32)]
    all_to_all x0 -> x3, starting transfers between devices: none -> 18.8 us  [the longest x1 10.6 us: local(): got = lax.all_to_all(part, REQ + SEQ, 0, 0, tiled=True)]
    ppermute x1 -> x4, waiting for transfers between devices: 2.98 us -> 18.3 us  [swap_cfg(): return lax.ppermute(value, 'cfg', [(0, 1), (1, 0)])]
    sub x2 -> x0, matrix products: 14.4 us -> none  [attend(): probs = jax.nn.softmax(scores, axis=-1).astype(jnp.bfloat16)]
  transfers between devices with their start and end apart: 8 -> 10, of which waited for: 8 -> 8; matrix products, arithmetic and copies ran while one was open for 2% -> 4% of each run, Pallas kernels for 0% -> 18%
where the time goes in v1:
time: 266 us; the launch traced here: 262 us
  waiting for transfers between devices  143 us (54%)
  Pallas kernels  59.8 us (22%)
  starting transfers between devices  25.7 us (10%)
  between operations  14 us (5%)
  matrix products  7.43 us (3%)
  other arithmetic  6.63 us (2%)
  local copies, waits for them, and re-layouts  4.63 us (2%)
    all_gather x1, waiting for transfers between devices, local(): lax.all_gather(jnp.stack([w_up, w_down])[None], REQ + SEQ, axis=0, tiled=...  83.7 us
    pallas_call x2, Pallas kernels, attention(): pl.pallas_call(lambda *refs: attn_kernel(seqs, rows, TXT_PAD, *refs), out...  33.3 us
    all_gather x1, waiting for transfers between devices, local(): tokens = lax.all_gather(mine, SEQ, axis=1, tiled=True)  31.3 us
    pallas_call x2, Pallas kernels, mlp(): pl.pallas_call(mlp_kernel, out_shape=jax.ShapeDtypeStruct((count, width),...  26.5 us
    ppermute x4, waiting for transfers between devices, swap_cfg(): return lax.ppermute(value, 'cfg', [(0, 1), (1, 0)])  18.3 us
    all_to_all x1, starting transfers between devices, local(): got = lax.all_to_all(part, REQ + SEQ, 0, 0, tiled=True)  10.6 us
    all_to_all x2, starting transfers between devices, local(): att = lax.all_to_all(att, SEQ, 0, 0, tiled=True).reshape(-1, rows)  8.17 us
    dot_general x4, matrix products, dot(): return lax.dot_general(a, b, dims, preferred_element_type=jnp.float32)  7.43 us
  transfers between devices with their start and end apart: 10, of which 8 were waited for; matrix products, arithmetic and copies ran while one was open for 4% of the time, Pallas kernels for 18%

profile of v1, /device:TPU:70, one launch (start us, length us, event | category | flops | bytes accessed | tf_op | source)
XLA Modules:
  0.0 261.6 jit_solution(14310087762561814005)
XLA Ops:
  7.3 2.5 maximum_maximum_fusion
  12.5 10.6 %all-to-all-start = ((f32[64,4,128]{2,1,0:T(4,128)}), f32[64,4,128]{2,1,0:T(4,128)S(1)}, u32[]{:S(2)}, u32[]{:S(2)}) async-start(f32[64,4,128]{2,1,0:T(4,128)} %bitcast.2), calls=%async_computation | async-start | bytes 262144 | tf_op jit(solution)/shard_map/all_to_all | solution.py:197
  23.3 5.6 %all-to-all-done = f32[64,4,128]{2,1,0:T(4,128)S(1)} async-done(((f32[64,4,128]{2,1,0:T(4,128)}), f32[64,4,128]{2,1,0:T(4,128)S(1)}, u32[]{:S(2)}, u32[]{:S(2)}) %all-to-all-start) | async-done | bytes 131104 | tf_op jit(solution)/shard_map/all_to_all | solution.py:197
  29.3 31.3 %all-gather.5.cloned.1.call-done.refs_0_ = bf16[2,1280,1536]{2,1,0:T(8,128)(2,1)} async-done(((bf16[2,160,1536]{2,1,0:T(8,128)(2,1)}), bf16[2,1280,1536]{2,1,0:T(8,128)(2,1)}) %all-gather.5.cloned.1.call-update) | async-done | bytes 7864336 | tf_op jit(solution)/shard_map/all_gather | solution.py:188
  60.6 1.5 copy-done.2
  62.0 16.7 %attn.2 = bf16[8,192,128]{2,1,0:T(8,128)(2,1)} custom-call(bf16[2,1280,1536]{2,1,0:T(8,128)(2,1)} %all-gather.5.cloned.1.call-done.refs_0_, f32[2,10,1536]{2,1,0:T(8,128)S(1)} %reshape.205.refs_1_, f32[2,256,1]{2,1,0:T(8,128)S(1)} %and_select_fusion.refs_2_, bf16[3,192,1536]{2,1,0:T(8,128)(2,1)S(1)} %copy-done.1, bf16[3,192,1536]{2,1,0:T(8,128)(2,1)S(1)} %copy-done.2), custom_call_target="tpu_custom_call" | custom-call | flops 1000000 | bytes 1000000 | tf_op jit(solution)/shard_map/attn/pallas_call | solution.py:89
  78.7 3.5 %all-to-all-start.1 = ((bf16[8,192,128]{2,1,0:T(8,128)(2,1)}), bf16[8,192,128]{2,1,0:T(8,128)(2,1)S(1)}, u32[]{:S(2)}, u32[]{:S(2)}) async-start(bf16[8,192,128]{2,1,0:T(8,128)(2,1)} %attn.2), calls=%async_computation.1 | async-start | bytes 786432 | tf_op jit(solution)/shard_map/all_to_all | solution.py:213
  82.4 1.5 copy-done.3
  83.8 16.6 %attn.3 = bf16[8,192,128]{2,1,0:T(8,128)(2,1)} custom-call(bf16[2,1280,1536]{2,1,0:T(8,128)(2,1)} %all-gather.5.cloned.1.call-done.refs_0_, f32[2,10,1536]{2,1,0:T(8,128)S(1)} %reshape.205.refs_1_, f32[2,256,1]{2,1,0:T(8,128)S(1)} %and_select_fusion.refs_2_, bf16[3,192,1536]{2,1,0:T(8,128)(2,1)S(1)} %copy-done.1, bf16[3,192,1536]{2,1,0:T(8,128)(2,1)S(1)} %copy-done.3), custom_call_target="tpu_custom_call" | custom-call | flops 1000000 | bytes 1000000 | tf_op jit(solution)/shard_map/attn/pallas_call | solution.py:89
  100.5 4.7 %all-to-all-start.2 = ((bf16[8,192,128]{2,1,0:T(8,128)(2,1)}), bf16[8,192,128]{2,1,0:T(8,128)(2,1)S(1)}, u32[]{:S(2)}, u32[]{:S(2)}) async-start(bf16[8,192,128]{2,1,0:T(8,128)(2,1)} %attn.3), calls=%async_computation.2 | async-start | bytes 786432 | tf_op jit(solution)/shard_map/all_to_all | solution.py:213
  105.2 3.4 %convert_reduce_fusion.1 = (f32[128]{0:T(128)S(1)}, bf16[128,1536]{1,0:T(8,128)(2,1)S(1)}) fusion(bf16[1536,128]{1,0:T(8,128)(2,1)S(1)} %bitcast.75, bf16[1536,1536]{1,0:T(8,128)(2,1)} %all-gather.7.cloned.1.call-done, f32[1536]{0:T(1024)S(1)} %get-tuple-element.7, bf16[1,2,128,1536]{3,2,1,0:T(8,128)(2,1)} %param.12), kind=kOutput, calls=%fused_computation.16 | convolution fusion | flops 605159296 | bytes 5904896 | tf_op jit(solution)/shard_map/dot_general | solution.py:21
  109.2 1.3 collective-permute-start
  110.6 3.6 %all-to-all-done.2 = bf16[8,192,128]{2,1,0:T(8,128)(2,1)S(1)} async-done(((bf16[8,192,128]{2,1,0:T(8,128)(2,1)}), bf16[8,192,128]{2,1,0:T(8,128)(2,1)S(1)}, u32[]{:S(2)}, u32[]{:S(2)}) %all-to-all-start.2) | async-done | bytes 393248 | tf_op jit(solution)/shard_map/all_to_all | solution.py:213
  114.1 3.4 %convert_reduce_fusion = (f32[128]{0:T(128)S(1)}, bf16[128,1536]{1,0:T(8,128)(2,1)S(1)}) fusion(bf16[1536,128]{1,0:T(8,128)(2,1)S(1)} %bitcast.76, bf16[1536,1536]{1,0:T(8,128)(2,1)} %all-gather.7.cloned.1.call-done, f32[1536]{0:T(1024)S(1)} %get-tuple-element.6, bf16[1,2,128,1536]{3,2,1,0:T(8,128)(2,1)S(1)} %copy-done.4), kind=kOutput, calls=%fused_computation.14 | convolution fusion | flops 605159296 | bytes 5904896 | tf_op jit(solution)/shard_map/dot_general | solution.py:21
  118.1 1.3 collective-permute-start.1
  119.5 3.8 %collective-permute-done = bf16[128,1536]{1,0:T(8,128)(2,1)S(1)} collective-permute-done((bf16[128,1536]{1,0:T(8,128)(2,1)S(1)}, bf16[128,1536]{1,0:T(8,128)(2,1)S(1)}, u32[]{:S(2)}, u32[]{:S(2)}) %collective-permute-start) | collective-permute-done | bytes 393248 | tf_op jit(solution)/shard_map/ppermute | solution.py:161
  123.3 8.0 %collective-permute-done.1 = bf16[128,1536]{1,0:T(8,128)(2,1)S(1)} collective-permute-done((bf16[128,1536]{1,0:T(8,128)(2,1)S(1)}, bf16[128,1536]{1,0:T(8,128)(2,1)S(1)}, u32[]{:S(2)}, u32[]{:S(2)}) %collective-permute-start.1) | collective-permute-done | bytes 393248 | tf_op jit(solution)/shard_map/ppermute | solution.py:161
  131.4 83.7 %all-gather.9.cloned.1.call-done = bf16[128,48,1536]{2,1,0:T(8,128)(2,1)} async-done(((bf16[2,48,1536]{2,1,0:T(8,128)(2,1)}), bf16[128,48,1536]{2,1,0:T(8,128)(2,1)}) %all-gather.9.cloned.1.call-update) | async-done | bytes 18874384 | tf_op jit(solution)/shard_map/all_gather | solution.py:202
  215.1 13.2 %mlp.3 = bf16[256,1536]{1,0:T(8,128)(2,1)S(1)} custom-call(bf16[256,1536]{1,0:T(8,128)(2,1)S(1)} %pad_maximum_fusion.2.x_ref, bf16[64,2,48,1536]{3,2,1,0:T(8,128)(2,1)} %bitcast.67, bf16[64,2,48,1536]{3,2,1,0:T(8,128)(2,1)} %bitcast.68), custom_call_target="tpu_custom_call" | custom-call | flops 4831838208 | bytes 18874368 | tf_op jit(solution)/shard_map/mlp/pallas_call | solution.py:139
  228.4 2.2 collective-permute-start.2
  230.7 13.3 %mlp.2 = f32[256,1536]{1,0:T(8,128)S(1)} custom-call(bf16[256,1536]{1,0:T(8,128)(2,1)S(1)} %pad_maximum_fusion.1.x_ref, bf16[64,2,48,1536]{3,2,1,0:T(8,128)(2,1)} %bitcast.69, bf16[64,2,48,1536]{3,2,1,0:T(8,128)(2,1)} %bitcast.70), custom_call_target="tpu_custom_call" | custom-call | flops 4831838208 | bytes 18874368 | tf_op jit(solution)/shard_map/mlp/pallas_call | solution.py:139
  244.0 4.5 %collective-permute-done.2 = bf16[256,1536]{1,0:T(8,128)(2,1)S(1)} collective-permute-done((bf16[256,1536]{1,0:T(8,128)(2,1)S(1)}, bf16[256,1536]{1,0:T(8,128)(2,1)S(1)}, u32[]{:S(2)}, u32[]{:S(2)}) %collective-permute-start.2) | collective-permute-done | bytes 786464 | tf_op jit(solution)/shard_map/ppermute | solution.py:161
  250.6 1.8 collective-permute-start.3
  252.4 2.0 collective-permute-done.3
  (65 shorter events, 7.3 us)
Async XLA Ops:
  7.2 4.3 %copy-start = (bf16[240,1536]{1,0:T(8,128)(2,1)S(1)}, bf16[240,1536]{1,0:T(8,128)(2,1)}, u32[]{:S(2)}) copy-start(bf16[240,1536]{1,0:T(8,128)(2,1)} %param.17) | copy-start | bytes 2211844
  7.2 53.4 %all-gather.5.cloned.1.call-start = ((), (), s32[]{:S(2)}) async-start(), calls=%async_computation.3 | async-start | bytes 8847360 | tf_op jit(solution)/shard_map/all_gather | solution.py:188
  7.3 3.4 %copy-start.6 = (bf16[48,1536]{1,0:T(8,128)(2,1)S(1)}, bf16[48,1536]{1,0:T(8,128)(2,1)}, u32[]{:S(2)}) copy-start(bf16[48,1536]{1,0:T(8,128)(2,1)} %param.22) | copy-start | bytes 442372
  7.3 3.4 %copy-start.7 = (bf16[48,1536]{1,0:T(8,128)(2,1)S(1)}, bf16[48,1536]{1,0:T(8,128)(2,1)}, u32[]{:S(2)}) copy-start(bf16[48,1536]{1,0:T(8,128)(2,1)} %param.21) | copy-start | bytes 442372
  9.9 1.6 copy-start.8
  9.9 13.3 %copy-start.10 = (s32[1,2]{1,0:T(1,128)S(1)}, s32[1,2]{1,0:T(1,128)}, u32[]{:S(2)}) copy-start(s32[1,2]{1,0:T(1,128)} %param.15) | copy-start | bytes 28
  9.9 95.3 %all-gather.7.cloned.1.call-start = ((), (), s32[]{:S(2)}) async-start(), calls=%async_computation.4 | async-start | bytes 5308416 | tf_op jit(solution)/shard_map/all_gather | solution.py:201
  10.6 204.5 %all-gather.9.cloned.1.call-start = ((), (), s32[]{:S(2)}) async-start(), calls=%async_computation.5 | async-start | bytes 19169280 | tf_op jit(solution)/shard_map/all_gather | solution.py:202
  11.5 49.1 %copy-start.1 = (bf16[3,192,1536]{2,1,0:T(8,128)(2,1)S(1)}, bf16[3,192,1536]{2,1,0:T(8,128)(2,1)}, u32[]{:S(2)}) copy-start(bf16[3,192,1536]{2,1,0:T(8,128)(2,1)} %refs_3_.3) | copy-start | bytes 5308420
  12.5 16.5 %all-to-all-start = ((f32[64,4,128]{2,1,0:T(4,128)}), f32[64,4,128]{2,1,0:T(4,128)S(1)}, u32[]{:S(2)}, u32[]{:S(2)}) async-start(f32[64,4,128]{2,1,0:T(4,128)} %bitcast.2), calls=%async_computation | async-start | bytes 262144 | tf_op jit(solution)/shard_map/all_to_all | solution.py:197
  60.6 1.5 copy-start.2
  78.7 21.7 %all-to-all-start.1 = ((bf16[8,192,128]{2,1,0:T(8,128)(2,1)}), bf16[8,192,128]{2,1,0:T(8,128)(2,1)S(1)}, u32[]{:S(2)}, u32[]{:S(2)}) async-start(bf16[8,192,128]{2,1,0:T(8,128)(2,1)} %attn.2), calls=%async_computation.1 | async-start | bytes 786432 | tf_op jit(solution)/shard_map/all_to_all | solution.py:213
  82.4 1.5 copy-start.3
  100.5 13.7 %all-to-all-start.2 = ((bf16[8,192,128]{2,1,0:T(8,128)(2,1)}), bf16[8,192,128]{2,1,0:T(8,128)(2,1)S(1)}, u32[]{:S(2)}, u32[]{:S(2)}) async-start(bf16[8,192,128]{2,1,0:T(8,128)(2,1)} %attn.3), calls=%async_computation.2 | async-start | bytes 786432 | tf_op jit(solution)/shard_map/all_to_all | solution.py:213
  105.2 8.9 %copy-start.4 = (bf16[1,2,128,1536]{3,2,1,0:T(8,128)(2,1)S(1)}, bf16[1,2,128,1536]{3,2,1,0:T(8,128)(2,1)}, u32[]{:S(2)}) copy-start(bf16[1,2,128,1536]{3,2,1,0:T(8,128)(2,1)} %param.12) | copy-start | bytes 2359300
  109.2 14.1 %collective-permute-start = (bf16[128,1536]{1,0:T(8,128)(2,1)S(1)}, bf16[128,1536]{1,0:T(8,128)(2,1)S(1)}, u32[]{:S(2)}, u32[]{:S(2)}) collective-permute-start(bf16[128,1536]{1,0:T(8,128)(2,1)S(1)} %fusion.16), channel_id=1, source_target_pairs={{0,64},{64,0},{1,65},{65,1},{2,66},{66,2},{3,67},{67,3},{4,68},{68... | collective-permute-start | bytes 1179656 | tf_op jit(solution)/shard_map/ppermute | solution.py:161
  118.1 13.2 %collective-permute-start.1 = (bf16[128,1536]{1,0:T(8,128)(2,1)S(1)}, bf16[128,1536]{1,0:T(8,128)(2,1)S(1)}, u32[]{:S(2)}, u32[]{:S(2)}) collective-permute-start(bf16[128,1536]{1,0:T(8,128)(2,1)S(1)} %fusion.12), channel_id=1, source_target_pairs={{0,64},{64,0},{1,65},{65,1},{2,66},{66,2},{3,67},{67,3},{4,68},{68... | collective-permute-start | bytes 1179656 | tf_op jit(solution)/shard_map/ppermute | solution.py:161
  228.4 20.2 %collective-permute-start.2 = (bf16[256,1536]{1,0:T(8,128)(2,1)S(1)}, bf16[256,1536]{1,0:T(8,128)(2,1)S(1)}, u32[]{:S(2)}, u32[]{:S(2)}) collective-permute-start(bf16[256,1536]{1,0:T(8,128)(2,1)S(1)} %mlp.3), channel_id=1, source_target_pairs={{0,64},{64,0},{1,65},{65,1},{2,66},{66,2},{3,67},{67,3},{4,68},{68... | collective-permute-start | bytes 2359304 | tf_op jit(solution)/shard_map/ppermute | solution.py:161
  249.3 0.9 copy-start.5
  249.3 5.1 %copy-start.9 = (f32[2,128,32]{1,2,0:T(8,128)S(1)}, f32[2,128,32]{1,2,0:T(8,128)}, u32[]{:S(2)}) copy-start(f32[2,128,32]{1,2,0:T(8,128)} %param.16) | copy-start | bytes 98308
  250.6 3.8 %collective-permute-start.3 = (bf16[2,128,32]{1,2,0:T(8,128)(2,1)S(1)}, bf16[2,128,32]{1,2,0:T(8,128)(2,1)S(1)}, u32[]{:S(2)}, u32[]{:S(2)}) collective-permute-start(bf16[2,128,32]{1,2,0:T(8,128)(2,1)S(1)} %select_convert_fusion), channel_id=1, source_target_pairs={{0,64},{64,0},{1,65},{65,1},{2,66},{66,2},{3,67},{67,3},{4,68},{68... | collective-permute-start | bytes 49160 | tf_op jit(solution)/shard_map/ppermute | solution.py:161
Sparse Core Ops, SparseCore 0:
  10.0 50.5 all-gather.4
  62.2 38.6 all-gather.6
  104.0 111.0 all-gather.8

commit v2 on v1

v2 whole, which is shorter than its diff:
```python
import math

import jax
import jax.numpy as jnp
import numpy as np
from jax import lax
from jax.experimental import pallas as pl
from jax.experimental.pallas import tpu as pltpu
from jax.sharding import Mesh
from jax.sharding import PartitionSpec as P

HEAD = 64
SEQ = ("y", "core")
REQ = ("zhi", "x")
NT = (((1,), (1,)), ((), ()))
NN = (((1,), (0,)), ((), ()))
TN = (((0,), (0,)), ((), ()))
TXT_PAD = 32
CHUNK = 32


def dot(a, b, dims):
    return lax.dot_general(a, b, dims, preferred_element_type=jnp.float32)


def layer_norm(value):
    mean = jnp.mean(value, axis=-1, keepdims=True)
    centered = value - mean
    spread = jnp.mean(centered * centered, axis=-1, keepdims=True)
    return centered * lax.rsqrt(spread + 1e-06)


def attn_kernel(idx_ref, *refs):
    *pieces, mod_ref, bias_ref, wi_ref, wt_ref, out_ref, ai, at, k_s, v_s, q_s = refs
    count = len(pieces)
    rows = pieces[0].shape[0] - TXT_PAD
    img = count * rows
    keys = img + count * TXT_PAD

    def modulated(part, scale, shift):
        normed = layer_norm(part.astype(jnp.float32))
        return (normed * (1.0 + mod_ref[0, scale : scale + 1, :]) + mod_ref[0, shift : shift + 1, :]).astype(
            jnp.bfloat16
        )

    for s, piece in enumerate(pieces):

        def one(i, carry, s=s, piece=piece):
            at_row = pl.multiple_of(i * CHUNK, CHUNK)
            ai[pl.ds(pl.multiple_of(s * rows + i * CHUNK, CHUNK), CHUNK), :] = modulated(
                piece[pl.ds(at_row, CHUNK), :], 1, 0
            )
            return carry

        lax.fori_loop(0, rows // CHUNK, one, 0)
        at[s * TXT_PAD : (s + 1) * TXT_PAD, :] = modulated(piece[rows : rows + TXT_PAD, :], 7, 6)
    heads = wi_ref.shape[1] // HEAD
    a_img, a_txt = ai[...], at[...]
    k_s[0:img, :] = dot(a_img, wi_ref[1], NT).astype(jnp.bfloat16)
    k_s[img:keys, :] = dot(a_txt, wt_ref[1], NT).astype(jnp.bfloat16)
    q_s[...] = (dot(wi_ref[0], a_img, NT) * (HEAD ** (-0.5) * math.log2(math.e))).astype(jnp.bfloat16)
    v_img = dot(wi_ref[2], a_img, NT).astype(jnp.bfloat16)
    v_txt = dot(wt_ref[2], a_txt, NT).astype(jnp.bfloat16)
    ones = jnp.ones((16, keys), jnp.bfloat16)
    for h in range(heads):
        v_s[h, 0:HEAD, 0:img] = v_img[h * HEAD : (h + 1) * HEAD, :]
        v_s[h, 0:HEAD, img:keys] = v_txt[h * HEAD : (h + 1) * HEAD, :]
        v_s[h, HEAD : HEAD + 16, :] = ones
    step = 2 * rows

    def some_queries(c, carry):
        at_query = pl.multiple_of(c * step, step)
        for h in range(heads):
            parts = []
            if h:
                parts.append(jnp.zeros((h * HEAD, step), jnp.bfloat16))
            parts.append(q_s[h * HEAD : (h + 1) * HEAD, pl.ds(at_query, step)])
            if h + 1 < heads:
                parts.append(jnp.zeros(((heads - 1 - h) * HEAD, step), jnp.bfloat16))
            q_h = jnp.concatenate(parts, axis=0)
            s_img = dot(k_s[0:img, :], q_h, NN)
            s_txt = dot(k_s[img:keys, :], q_h, NN) + bias_ref[0]
            top = jnp.maximum(
                jnp.max(s_img, axis=0, keepdims=True), jnp.max(s_txt, axis=0, keepdims=True)
            )
            p_img = jnp.exp2(s_img - top).astype(jnp.bfloat16)
            p_txt = jnp.exp2(s_txt - top).astype(jnp.bfloat16)
            o = dot(v_s[h, :, 0:img], p_img, NN) + dot(v_s[h, :, img:keys], p_txt, NN)
            o = (o[0:HEAD] / o[HEAD : HEAD + 1]).astype(jnp.bfloat16)
            for i in range(2):
                out_ref[idx_ref[2 * c + i], h * HEAD : (h + 1) * HEAD, :] = o[:, i * rows : (i + 1) * rows]
        return carry

    lax.fori_loop(0, img // step, some_queries, 0)


def attention(prompt, owners, pieces, mod, bias, w_img, w_txt):
    count = len(pieces)
    block, depth = pieces[0].shape
    rows = block - TXT_PAD
    width = w_img.shape[1]
    heads = width // HEAD
    keys = count * block
    once = lambda *zeros: (lambda i, owners: zeros)
    return pl.pallas_call(
        attn_kernel,
        out_shape=jax.ShapeDtypeStruct((count, width, rows), jnp.bfloat16),
        grid_spec=pltpu.PrefetchScalarGridSpec(
            num_scalar_prefetch=1,
            grid=(1,),
            in_specs=[pl.BlockSpec((block, depth), once(0, 0)) for _ in pieces]
            + [
                pl.BlockSpec((1, 10, depth), once(prompt, 0, 0)),
                pl.BlockSpec((1, count * TXT_PAD, 1), once(prompt, 0, 0)),
                pl.BlockSpec(w_img.shape, once(0, 0, 0)),
                pl.BlockSpec(w_txt.shape, once(0, 0, 0)),
            ],
            out_specs=pl.BlockSpec((count, width, rows), once(0, 0, 0)),
            scratch_shapes=[
                pltpu.VMEM((count * rows, depth), jnp.bfloat16),
                pltpu.VMEM((count * TXT_PAD, depth), jnp.bfloat16),
                pltpu.VMEM((keys, width), jnp.bfloat16),
                pltpu.VMEM((heads, HEAD + 16, keys), jnp.bfloat16),
                pltpu.VMEM((width, count * rows), jnp.bfloat16),
            ],
        ),
        compiler_params=pltpu.CompilerParams(vmem_limit_bytes=48 << 20),
        cost_estimate=pl.CostEstimate(flops=8000000000, bytes_accessed=8000000, transcendentals=0),
        name="attn",
    )(owners, *pieces, mod, bias, w_img, w_txt)


def proj_kernel(idx_ref, att_ref, *refs):
    *parts, img_ref, mod_ref, resid_ref, normed_ref = refs
    total = None
    for s, part in enumerate(parts):
        term = dot(att_ref[idx_ref[s]], part[...], TN)
        total = term if total is None else total + term
    one = (img_ref[0, 0].astype(jnp.float32) + mod_ref[0, 2:3, :] * total).astype(jnp.bfloat16)
    resid_ref[...] = one
    normed = layer_norm(one.astype(jnp.float32)) * (1.0 + mod_ref[0, 4:5, :]) + mod_ref[0, 3:4, :]
    normed_ref[...] = normed.astype(jnp.bfloat16)


def project(prompt, owners, att, parts, img_state, mod):
    rows, depth = img_state.shape[2:]
    once = lambda *zeros: (lambda i, owners: zeros)
    return pl.pallas_call(
        proj_kernel,
        out_shape=[jax.ShapeDtypeStruct((rows, depth), jnp.bfloat16)] * 2,
        grid_spec=pltpu.PrefetchScalarGridSpec(
            num_scalar_prefetch=1,
            grid=(1,),
            in_specs=[pl.BlockSpec(att.shape, once(0, 0, 0))]
            + [pl.BlockSpec(part.shape, once(0, 0)) for part in parts]
            + [
                pl.BlockSpec((1, 1, rows, depth), once(0, prompt, 0, 0)),
                pl.BlockSpec((1, 10, depth), once(prompt, 0, 0)),
            ],
            out_specs=[pl.BlockSpec((rows, depth), once(0, 0))] * 2,
        ),
        compiler_params=pltpu.CompilerParams(vmem_limit_bytes=32 << 20),
        cost_estimate=pl.CostEstimate(flops=600000000, bytes_accessed=5000000, transcendentals=0),
        name="proj",
    )(owners, att, *parts, img_state, mod)


def mlp_kernel(*refs):
    *pieces, up_ref, down_ref, keep_ref, send_ref, x_s, acc = refs
    step = pl.program_id(0)
    depth = up_ref.shape[-1]
    rows = pieces[0].shape[0]

    @pl.when(step == 0)
    def _():
        for i, piece in enumerate(pieces):
            x_s[i * rows : (i + 1) * rows, :] = piece[...]

    up = up_ref[...].reshape(-1, depth)
    down = down_ref[...].reshape(-1, depth)
    hidden = jax.nn.gelu(dot(x_s[...], up, NT), approximate=True).astype(jnp.bfloat16)
    term = dot(hidden, down, NN)

    @pl.when(step == 0)
    def _():
        acc[...] = term

    @pl.when(step > 0)
    def _():
        acc[...] += term

    @pl.when(step == pl.num_programs(0) - 1)
    def _():
        half = keep_ref.shape[0]
        keep_ref[...] = acc[0:half, :]
        send_ref[...] = acc[half:, :].astype(jnp.bfloat16)


def mlp(pieces, weights):
    shards, _, units, width = weights.shape
    many = 8
    rows = pieces[0].shape[0]
    count = rows * len(pieces)
    half = count // 2
    return pl.pallas_call(
        mlp_kernel,
        out_shape=[
            jax.ShapeDtypeStruct((half, width), jnp.float32),
            jax.ShapeDtypeStruct((half, width), jnp.bfloat16),
        ],
        grid=(shards // many,),
        in_specs=[pl.BlockSpec((rows, width), lambda i: (0, 0)) for _ in pieces]
        + [
            pl.BlockSpec((many, 1, units, width), lambda i: (i, 0, 0, 0)),
            pl.BlockSpec((many, 1, units, width), lambda i: (i, 1, 0, 0)),
        ],
        out_specs=[pl.BlockSpec((half, width), lambda i: (0, 0))] * 2,
        scratch_shapes=[
            pltpu.VMEM((count, width), jnp.bfloat16),
            pltpu.VMEM((count, width), jnp.float32),
        ],
        compiler_params=pltpu.CompilerParams(vmem_limit_bytes=44 << 20),
        cost_estimate=pl.CostEstimate(
            flops=4 * count * shards * units * width,
            bytes_accessed=4 * shards * units * width,
            transcendentals=0,
        ),
        name="mlp",
    )(*pieces, weights, weights)


def shifted(value, axis, by):
    size = lax.axis_size(axis)
    return lax.ppermute(value, axis, [(i, (i + by) % size) for i in range(size)])


def swap(value, axis):
    return shifted(value, axis, 1)


def gathered(value, forward_up):
    below = shifted(value, "y", 1)
    above = shifted(value, "y", -1)
    far = shifted(below, "y", 1) if forward_up else shifted(above, "y", -1)
    same = [value, below, above, far]
    return same + [swap(block, "core") for block in same]


def local(
    img_state,
    txt_state,
    cond_vec,
    text_len,
    latent,
    w_mod,
    w_qkv_img,
    w_qkv_txt,
    w_attn_out,
    w_up,
    w_down,
    w_final,
):
    prompts = img_state.shape[1]
    rows = img_state.shape[2]
    width = img_state.shape[3]
    txt_rows = txt_state.shape[2]
    high = lax.axis_size("y")
    seqs = high * lax.axis_size("core")
    reqs = lax.axis_size("zhi") * lax.axis_size("x")
    everyone = reqs * seqs

    own = jnp.stack([w_up, w_down])[None]
    weights = lax.all_gather(
        jnp.concatenate([own, swap(own, "zhi")], axis=0), ("x", "y"), axis=0, tiled=True
    )

    padding = jnp.zeros((prompts, TXT_PAD - txt_rows, width), jnp.bfloat16)
    mine = jnp.concatenate([img_state[0], txt_state[0], padding], axis=1)
    tokens = [gathered(mine[p], p % 2 == 0) for p in range(prompts)]
    w_out = gathered(w_attn_out, True)

    cond_act = jax.nn.silu(cond_vec[0]).astype(jnp.bfloat16)
    part = dot(cond_act, w_mod, NT)
    cols = part.shape[1]
    lanes = -(-cols // 128) * 128
    part = jnp.pad(part, ((0, 0), (0, lanes - cols)))
    part = part.reshape(reqs, 1, prompts * lanes // 128, 128)
    part = jnp.broadcast_to(part, (reqs, seqs) + part.shape[2:]).reshape((everyone,) + part.shape[2:])
    got = lax.all_to_all(part, REQ + SEQ, 0, 0, tiled=True)
    got = got.reshape(everyone, prompts, lanes)[:, :, :cols]
    mod = jnp.swapaxes(got, 0, 1).reshape(prompts, 10, width)

    here, core = lax.axis_index("y"), lax.axis_index("core")
    level = (here + jnp.array([0, high - 1, 1, 2], jnp.int32)) % high
    owners = jnp.concatenate([2 * level + core, 2 * level + 1 - core]).astype(jnp.int32)
    inside = jnp.arange(TXT_PAD)
    index = owners[:, None] * txt_rows + inside[None, :]
    live = (inside < txt_rows)[None, None, :] & (index[None] < text_len[0][:, None, None])
    bias = jnp.where(live, 0.0, -1e30).astype(jnp.float32).reshape(prompts, seqs * TXT_PAD, 1)

    att = [
        attention(p, owners, tokens[p], mod, bias, w_qkv_img, w_qkv_txt) for p in range(prompts)
    ]
    att = [lax.all_to_all(a, SEQ, 0, 0, tiled=True) for a in att]
    resid, normed = zip(
        *[project(p, owners, att[p], w_out, img_state, mod) for p in range(prompts)]
    )
    other = [swap(n, "cfg") for n in normed]
    mate = [swap(n, "core") for n in normed]
    other_mate = [swap(n, "core") for n in other]
    keep, send = mlp(other + other_mate, weights)
    back = swap((keep + swap(send, "core").astype(jnp.float32)).astype(jnp.bfloat16), "cfg")
    keep, send = mlp(list(normed) + mate, weights)
    mlp_out = keep + swap(send, "core").astype(jnp.float32) + back.astype(jnp.float32)
    mlp_out = mlp_out.reshape(prompts, rows, width)
    resid_two = jnp.stack(resid).astype(jnp.float32) + mod[:, 5:6] * mlp_out
    final_in = (layer_norm(resid_two) * (1.0 + mod[:, 9:10]) + mod[:, 8:9]).astype(jnp.bfloat16)
    branch_vel = dot(final_in.reshape(prompts * rows, width), w_final, NN)
    branch_vel = branch_vel.reshape(prompts, rows, -1)
    half = latent.shape[2]
    branch = lax.axis_index("cfg")
    first = branch == 0
    low, upper = branch_vel[:, :, :half], branch_vel[:, :, half:]
    own_half = jnp.where(first, low, upper)
    partner = swap(jnp.where(first, upper, low).astype(jnp.bfloat16), "cfg").astype(jnp.float32)
    cond_vel = jnp.where(first, own_half, partner)
    uncond_vel = jnp.where(first, partner, own_half)
    velocity = uncond_vel + 4.5 * (cond_vel - uncond_vel)
    return velocity, latent - 0.04 * velocity


def solution(mesh):
    fine = Mesh(np.asarray(mesh.devices).reshape(2, 2, 4, 4, 2), ("cfg", "zhi", "x", "y", "core"))
    every = ("cfg",) + REQ + SEQ
    placed = (
        P("cfg", REQ, SEQ, None),
        P("cfg", REQ, SEQ, None),
        P("cfg", None, None),
        P("cfg", REQ),
        P(REQ, SEQ, "cfg"),
        P(REQ + SEQ, None),
        P(None, SEQ, None),
        P(None, SEQ, None),
        P(SEQ, None),
        P(every, None),
        P(every, None),
        P(),
    )
    return jax.shard_map(
        local,
        mesh=fine,
        in_specs=placed,
        out_specs=(P(REQ, SEQ, "cfg"), P(REQ, SEQ, "cfg")),
        check_vma=False,
    )
```

time: 266 us -> 251 us (0.944); the launches traced: 262 us -> 250 us
  waiting for transfers between devices: 143 us -> 87.6 us
  Pallas kernels: 59.8 us -> 80.1 us
  starting transfers between devices: 25.7 us -> 42.7 us
  local copies, waits for them, and re-layouts: 4.63 us -> 17.7 us
  matrix products: 7.43 us -> 0.62 us
    all_gather x3 -> x1, waiting for transfers between devices: 115 us -> 0.01 us  [local(): lax.all_gather(jnp.concatenate([own, swap(own, 'zhi')], axis=0), ('x', 'y...]
    ppermute x4 -> x32, waiting for transfers between devices: 18.3 us -> 85.9 us  [shifted(): lax.ppermute(value, axis, [(i, (i + by) % size) for i in range(size)])]
    pallas_call x4 -> x6, Pallas kernels: 59.8 us -> 80.1 us  [the longest x2 48.3 us: attention(): pl.pallas_call(attn_kernel, out_shape=jax.ShapeDtypeStruct((count, width,...]
    ppermute x4 -> x32, starting transfers between devices: 6.76 us -> 25.6 us  [shifted(): lax.ppermute(value, axis, [(i, (i + by) % size) for i in range(size)])]
    unnamed x24 -> x60, local copies, waits for them, and re-layouts: 3.56 us -> 14.7 us
    dot_general x4 -> x2, matrix products: 7.43 us -> 0.62 us  [dot(): return lax.dot_general(a, b, dims, preferred_element_type=jnp.float32)]
    all_to_all x1, waiting for transfers between devices: 5.63 us -> 0.01 us  [local(): got = lax.all_to_all(part, REQ + SEQ, 0, 0, tiled=True)]
  transfers between devices with their start and end apart: 10 -> 36, of which waited for: 8 -> 10; matrix products, arithmetic and copies ran while one was open for 4% -> 2% of each run, Pallas kernels for 18% -> 32%
where the time goes in v2:
time: 251 us; the launch traced here: 250 us
  waiting for transfers between devices  87.6 us (35%)
  Pallas kernels  80.1 us (32%)
  starting transfers between devices  42.7 us (17%)
  local copies, waits for them, and re-layouts  17.7 us (7%)
  between operations  14.4 us (6%)
  other arithmetic  6.6 us (3%)
    ppermute x32, waiting for transfers between devices, shifted(): lax.ppermute(value, axis, [(i, (i + by) % size) for i in range(size)])  85.9 us
    pallas_call x2, Pallas kernels, attention(): pl.pallas_call(attn_kernel, out_shape=jax.ShapeDtypeStruct((count, width,...  48.3 us
    ppermute x32, starting transfers between devices, shifted(): lax.ppermute(value, axis, [(i, (i + by) % size) for i in range(size)])  25.6 us
    pallas_call x2, Pallas kernels, mlp(): pl.pallas_call(mlp_kernel, out_shape=[jax.ShapeDtypeStruct((half, width),...  22.7 us
    unnamed x60, local copies, waits for them, and re-layouts  14.7 us
    pallas_call x2, Pallas kernels, project(): pl.pallas_call(proj_kernel, out_shape=[jax.ShapeDtypeStruct((rows, depth)...  9.06 us
    all_to_all x2, starting transfers between devices, local(): att = [lax.all_to_all(a, SEQ, 0, 0, tiled=True) for a in att]  8.81 us
    all_to_all x1, starting transfers between devices, local(): got = lax.all_to_all(part, REQ + SEQ, 0, 0, tiled=True)  8.21 us
  transfers between devices with their start and end apart: 36, of which 10 were waited for; matrix products, arithmetic and copies ran while one was open for 2% of the time, Pallas kernels for 32%

profile of v2, /device:TPU:70, one launch (start us, length us, event | category | flops | bytes accessed | tf_op | source)
XLA Modules:
  0.0 249.8 jit_solution(17632837279508140582)
XLA Ops:
  8.5 10.2 %collective-permute-done.23 = bf16[1,2,48,1536]{3,2,1,0:T(8,128)(2,1)S(1)} collective-permute-done((bf16[1,2,48,1536]{3,2,1,0:T(8,128)(2,1)S(1)}, bf16[1,2,48,1536]{3,2,1,0:T(8,128)(2,1)S(1)}, u32[]{:S(2)}, u32[]{:S(2)}) %collective-permute-start.23) | collective-permute-done | bytes 294944 | tf_op jit(solution)/shard_map/ppermute | solution.py:234
  23.8 2.9 %collective-permute-start.15 = (bf16[160,1536]{1,0:T(8,128)(2,1)S(1)}, bf16[160,1536]{1,0:T(8,128)(2,1)}, u32[]{:S(2)}, u32[]{:S(2)}) collective-permute-start(bf16[160,1536]{1,0:T(8,128)(2,1)S(1)} %get-tuple-element.26.refs_0_), channel_id=1, source_target_pairs={{0,6},{2,0},{4,2},{6,4},{1,7},{3,1},{5,3},{7,5},{8,14},{10,8},{12,... | collective-permute-start | bytes 1474568 | tf_op jit(solution)/shard_map/ppermute | solution.py:234
  27.7 8.2 %all-to-all-start = ((f32[64,4,128]{2,1,0:T(4,128)}), f32[64,4,128]{2,1,0:T(4,128)S(1)}, u32[]{:S(2)}, u32[]{:S(2)}) async-start(f32[64,4,128]{2,1,0:T(4,128)} %bitcast.4), calls=%async_computation | async-start | bytes 262144 | tf_op jit(solution)/shard_map/all_to_all | solution.py:289
  40.6 16.2 %collective-permute-done.14.refs_1_ = bf16[160,1536]{1,0:T(8,128)(2,1)} collective-permute-done((bf16[160,1536]{1,0:T(8,128)(2,1)S(1)}, bf16[160,1536]{1,0:T(8,128)(2,1)}, u32[]{:S(2)}, u32[]{:S(2)}) %collective-permute-start.14) | collective-permute-done | bytes 491552 | tf_op jit(solution)/shard_map/ppermute | solution.py:234
  58.2 1.7 collective-permute-start.16
  59.9 8.6 %collective-permute-done.2.refs_3_ = bf16[160,1536]{1,0:T(8,128)(2,1)} collective-permute-done((bf16[160,1536]{1,0:T(8,128)(2,1)}, bf16[160,1536]{1,0:T(8,128)(2,1)}, u32[]{:S(2)}, u32[]{:S(2)}) %collective-permute-start.2) | collective-permute-done | bytes 491552 | tf_op jit(solution)/shard_map/ppermute | solution.py:234
  71.5 20.2 %collective-permute-done.7.refs_1_ = bf16[192,1536]{1,0:T(8,128)(2,1)S(1)} collective-permute-done((bf16[192,1536]{1,0:T(8,128)(2,1)S(1)}, bf16[192,1536]{1,0:T(8,128)(2,1)S(1)}, u32[]{:S(2)}, u32[]{:S(2)}) %collective-permute-start.7) | collective-permute-done | bytes 589856 | tf_op jit(solution)/shard_map/ppermute | solution.py:234
  91.7 2.7 %collective-permute-start.8 = (bf16[192,1536]{1,0:T(8,128)(2,1)S(1)}, bf16[192,1536]{1,0:T(8,128)(2,1)S(1)}, u32[]{:S(2)}, u32[]{:S(2)}) collective-permute-start(bf16[192,1536]{1,0:T(8,128)(2,1)S(1)} %copy-done.2), channel_id=1, source_target_pairs={{0,6},{2,0},{4,2},{6,4},{1,7},{3,1},{5,3},{7,5},{8,14},{10,8},{12,... | collective-permute-start | bytes 1769480 | tf_op jit(solution)/shard_map/ppermute | solution.py:234
  97.3 24.3 %attn.2 = bf16[8,192,128]{2,1,0:T(8,128)(2,1)S(1)} custom-call(s32[8]{0:T(128)S(1)} %get-tuple-element.23.idx_ref, bf16[160,1536]{1,0:T(8,128)(2,1)S(1)} %copy-done.6, bf16[160,1536]{1,0:T(8,128)(2,1)} %collective-permute-done.refs_1_, bf16[160,1536]{1,0:T(8,128)(2,1)} %collective-permute-done.1.refs_2_, bf16[160,1536]{1,0:T(8,128)(2,1)} %collective-permute-done.2.refs_3_, ...), custom_call_target="tpu_custom_call" | custom-call | flops 8000000000 | bytes 8000000 | tf_op jit(solution)/shard_map/attn/pallas_call | solution.py:105
  122.3 4.1 %all-to-all-start.1 = ((bf16[8,192,128]{2,1,0:T(8,128)(2,1)}), bf16[8,192,128]{2,1,0:T(8,128)(2,1)}, u32[]{:S(2)}, u32[]{:S(2)}) async-start(bf16[8,192,128]{2,1,0:T(8,128)(2,1)} %copy-done.7), calls=%async_computation.1 | async-start | bytes 786432 | tf_op jit(solution)/shard_map/all_to_all | solution.py:304
  130.6 24.0 %attn.3 = bf16[8,192,128]{2,1,0:T(8,128)(2,1)S(1)} custom-call(s32[8]{0:T(128)S(1)} %get-tuple-element.23.idx_ref, bf16[160,1536]{1,0:T(8,128)(2,1)S(1)} %copy-done.4, bf16[160,1536]{1,0:T(8,128)(2,1)} %collective-permute-done.14.refs_1_, bf16[160,1536]{1,0:T(8,128)(2,1)} %collective-permute-done.15.refs_2_, ...), custom_call_target="tpu_custom_call" | custom-call | flops 8000000000 | bytes 8000000 | tf_op jit(solution)/shard_map/attn/pallas_call | solution.py:105
  155.3 4.7 %all-to-all-start.2 = ((bf16[8,192,128]{2,1,0:T(8,128)(2,1)}), bf16[8,192,128]{2,1,0:T(8,128)(2,1)}, u32[]{:S(2)}, u32[]{:S(2)}) async-start(bf16[8,192,128]{2,1,0:T(8,128)(2,1)} %copy-done.8), calls=%async_computation.2 | async-start | bytes 786432 | tf_op jit(solution)/shard_map/all_to_all | solution.py:304
  160.1 4.5 %proj.2 = (bf16[128,1536]{1,0:T(8,128)(2,1)S(1)}, bf16[128,1536]{1,0:T(8,128)(2,1)}) custom-call(s32[8]{0:T(128)S(1)} %get-tuple-element.23.idx_ref, bf16[8,192,128]{2,1,0:T(8,128)(2,1)} %all-to-all-done.1.att_ref, bf16[192,1536]{1,0:T(8,128)(2,1)S(1)} %copy-done.2, bf16[192,1536]{1,0:T(8,128)(2,1)S(1)} %collective-permute-done.7.refs_1_, ...), custom_call_target="tpu_custom_call" | custom-call | flops 600000000 | bytes 5000000 | tf_op jit(solution)/shard_map/proj/pallas_call | solution.py:148
  165.4 2.0 collective-permute-start.25
  167.3 1.7 all-to-all-done.2.att_ref
  169.1 4.5 %proj.3 = (bf16[128,1536]{1,0:T(8,128)(2,1)S(1)}, bf16[128,1536]{1,0:T(8,128)(2,1)}) custom-call(s32[8]{0:T(128)S(1)} %get-tuple-element.23.idx_ref, bf16[8,192,128]{2,1,0:T(8,128)(2,1)} %all-to-all-done.2.att_ref, bf16[192,1536]{1,0:T(8,128)(2,1)S(1)} %copy-done.2, bf16[192,1536]{1,0:T(8,128)(2,1)S(1)} %collective-permute-done.7.refs_1_, ...), custom_call_target="tpu_custom_call" | custom-call | flops 600000000 | bytes 5000000 | tf_op jit(solution)/shard_map/proj/pallas_call | solution.py:148
  174.4 2.0 collective-permute-start.26
  177.7 8.1 %collective-permute-done.26.refs_1_ = bf16[128,1536]{1,0:T(8,128)(2,1)S(1)} collective-permute-done((bf16[128,1536]{1,0:T(8,128)(2,1)}, bf16[128,1536]{1,0:T(8,128)(2,1)S(1)}, u32[]{:S(2)}, u32[]{:S(2)}) %collective-permute-start.26) | collective-permute-done | bytes 393248 | tf_op jit(solution)/shard_map/ppermute | solution.py:234
  191.5 11.7 %mlp.3 = (f32[256,1536]{1,0:T(8,128)S(1)}, bf16[256,1536]{1,0:T(8,128)(2,1)}) custom-call(bf16[128,1536]{1,0:T(8,128)(2,1)} %collective-permute-done.25.refs_0_, bf16[128,1536]{1,0:T(8,128)(2,1)S(1)} %copy-done.14, bf16[128,1536]{1,0:T(8,128)(2,1)S(1)} %copy-done.16, bf16[128,1536]{1,0:T(8,128)(2,1)S(1)} %copy-done.18, ...), custom_call_target="tpu_custom_call" | custom-call | flops 4831838208 | bytes 9437184 | tf_op jit(solution)/shard_map/mlp/pallas_call | solution.py:205
  203.8 11.0 %mlp.2 = (f32[256,1536]{1,0:T(8,128)S(1)}, bf16[256,1536]{1,0:T(8,128)(2,1)S(1)}) custom-call(bf16[128,1536]{1,0:T(8,128)(2,1)} %get-tuple-element.12.refs_0_, bf16[128,1536]{1,0:T(8,128)(2,1)} %get-tuple-element.13.refs_1_, bf16[128,1536]{1,0:T(8,128)(2,1)S(1)} %collective-permute-done.21.refs_2_, bf16[128,1536]{1,0:T(8,128)(2,1)S(1)} %collective-permute-done.22.refs_3_, ...), custom_call_target="tpu_custom_call" | custom-call | flops 4831838208 | bytes 9437184 | tf_op jit(solution)/shard_map/mlp/pallas_call | solution.py:205
  216.3 1.8 collective-permute-start.30
  218.3 18.0 %collective-permute-done.30 = bf16[256,1536]{1,0:T(8,128)(2,1)S(1)} collective-permute-done((bf16[256,1536]{1,0:T(8,128)(2,1)S(1)}, bf16[256,1536]{1,0:T(8,128)(2,1)S(1)}, u32[]{:S(2)}, u32[]{:S(2)}) %collective-permute-start.30) | collective-permute-done | bytes 786464 | tf_op jit(solution)/shard_map/ppermute | solution.py:234
  238.4 1.8 collective-permute-start.31
  240.3 2.0 collective-permute-done.31
  (152 shorter events, 38.2 us)
Async XLA Ops:
  7.2 181.3 %all-gather.2.cloned.1.call-start = ((), (), s32[]{:S(2)}) async-start(), calls=%async_computation.3 | async-start | bytes 10027008 | tf_op jit(solution)/shard_map/all_gather | solution.py:273
  23.5 33.4 %collective-permute-start.14 = (bf16[160,1536]{1,0:T(8,128)(2,1)S(1)}, bf16[160,1536]{1,0:T(8,128)(2,1)}, u32[]{:S(2)}, u32[]{:S(2)}) collective-permute-start(bf16[160,1536]{1,0:T(8,128)(2,1)S(1)} %get-tuple-element.26.refs_0_), channel_id=1, source_target_pairs={{0,2},{2,4},{4,6},{6,0},{1,3},{3,5},{5,7},{7,1},{8,10},{10,12},{12... | collective-permute-start | bytes 1474568 | tf_op jit(solution)/shard_map/ppermute | solution.py:234
  23.8 33.0 %collective-permute-start.15 = (bf16[160,1536]{1,0:T(8,128)(2,1)S(1)}, bf16[160,1536]{1,0:T(8,128)(2,1)}, u32[]{:S(2)}, u32[]{:S(2)}) collective-permute-start(bf16[160,1536]{1,0:T(8,128)(2,1)S(1)} %get-tuple-element.26.refs_0_), channel_id=1, source_target_pairs={{0,6},{2,0},{4,2},{6,4},{1,7},{3,1},{5,3},{7,5},{8,14},{10,8},{12,... | collective-permute-start | bytes 1474568 | tf_op jit(solution)/shard_map/ppermute | solution.py:234
  27.7 41.9 %all-to-all-start = ((f32[64,4,128]{2,1,0:T(4,128)}), f32[64,4,128]{2,1,0:T(4,128)S(1)}, u32[]{:S(2)}, u32[]{:S(2)}) async-start(f32[64,4,128]{2,1,0:T(4,128)} %bitcast.4), calls=%async_computation | async-start | bytes 262144 | tf_op jit(solution)/shard_map/all_to_all | solution.py:289
  36.0 21.4 %collective-permute-start.17 = (bf16[160,1536]{1,0:T(8,128)(2,1)S(1)}, bf16[160,1536]{1,0:T(8,128)(2,1)S(1)}, u32[]{:S(2)}, u32[]{:S(2)}) collective-permute-start(bf16[160,1536]{1,0:T(8,128)(2,1)S(1)} %get-tuple-element.26.refs_0_), channel_id=1, source_target_pairs={{0,1},{1,0},{2,3},{3,2},{4,5},{5,4},{6,7},{7,6},{8,9},{9,8},{10,11... | collective-permute-start | bytes 1474568 | tf_op jit(solution)/shard_map/ppermute | solution.py:234
  37.3 31.2 %collective-permute-start.2 = (bf16[160,1536]{1,0:T(8,128)(2,1)}, bf16[160,1536]{1,0:T(8,128)(2,1)}, u32[]{:S(2)}, u32[]{:S(2)}) collective-permute-start(bf16[160,1536]{1,0:T(8,128)(2,1)} %collective-permute-done.refs_1_), channel_id=1, source_target_pairs={{0,2},{2,4},{4,6},{6,0},{1,3},{3,5},{5,7},{7,1},{8,10},{10,12},{12... | collective-permute-start | bytes 1474568 | tf_op jit(solution)/shard_map/ppermute | solution.py:234
  39.1 52.6 %collective-permute-start.7 = (bf16[192,1536]{1,0:T(8,128)(2,1)S(1)}, bf16[192,1536]{1,0:T(8,128)(2,1)S(1)}, u32[]{:S(2)}, u32[]{:S(2)}) collective-permute-start(bf16[192,1536]{1,0:T(8,128)(2,1)S(1)} %copy-done.2), channel_id=1, source_target_pairs={{0,2},{2,4},{4,6},{6,0},{1,3},{3,5},{5,7},{7,1},{8,10},{10,12},{12... | collective-permute-start | bytes 1769480 | tf_op jit(solution)/shard_map/ppermute | solution.py:234
  56.9 37.5 %collective-permute-start.4 = (bf16[160,1536]{1,0:T(8,128)(2,1)}, bf16[160,1536]{1,0:T(8,128)(2,1)}, u32[]{:S(2)}, u32[]{:S(2)}) collective-permute-start(bf16[160,1536]{1,0:T(8,128)(2,1)} %collective-permute-done.refs_1_), channel_id=1, source_target_pairs={{0,1},{1,0},{2,3},{3,2},{4,5},{5,4},{6,7},{7,6},{8,9},{9,8},{10,11... | collective-permute-start | bytes 1474568 | tf_op jit(solution)/shard_map/ppermute | solution.py:234
  56.9 37.5 %collective-permute-start.5 = (bf16[160,1536]{1,0:T(8,128)(2,1)}, bf16[160,1536]{1,0:T(8,128)(2,1)}, u32[]{:S(2)}, u32[]{:S(2)}) collective-permute-start(bf16[160,1536]{1,0:T(8,128)(2,1)} %collective-permute-done.1.refs_2_), channel_id=1, source_target_pairs={{0,1},{1,0},{2,3},{3,2},{4,5},{5,4},{6,7},{7,6},{8,9},{9,8},{10,11... | collective-permute-start | bytes 1474568 | tf_op jit(solution)/shard_map/ppermute | solution.py:234
  58.2 36.8 %collective-permute-start.16 = (bf16[160,1536]{1,0:T(8,128)(2,1)}, bf16[160,1536]{1,0:T(8,128)(2,1)}, u32[]{:S(2)}, u32[]{:S(2)}) collective-permute-start(bf16[160,1536]{1,0:T(8,128)(2,1)} %collective-permute-done.15.refs_2_), channel_id=1, source_target_pairs={{0,6},{2,0},{4,2},{6,4},{1,7},{3,1},{5,3},{7,5},{8,14},{10,8},{12,... | collective-permute-start | bytes 1474568 | tf_op jit(solution)/shard_map/ppermute | solution.py:234
  68.5 26.4 %collective-permute-start.6 = (bf16[160,1536]{1,0:T(8,128)(2,1)}, bf16[160,1536]{1,0:T(8,128)(2,1)}, u32[]{:S(2)}, u32[]{:S(2)}) collective-permute-start(bf16[160,1536]{1,0:T(8,128)(2,1)} %collective-permute-done.2.refs_3_), channel_id=1, source_target_pairs={{0,1},{1,0},{2,3},{3,2},{4,5},{5,4},{6,7},{7,6},{8,9},{9,8},{10,11... | collective-permute-start | bytes 1474568 | tf_op jit(solution)/shard_map/ppermute | solution.py:234
  91.7 34.8 %collective-permute-start.8 = (bf16[192,1536]{1,0:T(8,128)(2,1)S(1)}, bf16[192,1536]{1,0:T(8,128)(2,1)S(1)}, u32[]{:S(2)}, u32[]{:S(2)}) collective-permute-start(bf16[192,1536]{1,0:T(8,128)(2,1)S(1)} %copy-done.2), channel_id=1, source_target_pairs={{0,6},{2,0},{4,2},{6,4},{1,7},{3,1},{5,3},{7,5},{8,14},{10,8},{12,... | collective-permute-start | bytes 1769480 | tf_op jit(solution)/shard_map/ppermute | solution.py:234
  94.4 32.7 %collective-permute-start.19 = (bf16[160,1536]{1,0:T(8,128)(2,1)}, bf16[160,1536]{1,0:T(8,128)(2,1)}, u32[]{:S(2)}, u32[]{:S(2)}) collective-permute-start(bf16[160,1536]{1,0:T(8,128)(2,1)} %collective-permute-done.15.refs_2_), channel_id=1, source_target_pairs={{0,1},{1,0},{2,3},{3,2},{4,5},{5,4},{6,7},{7,6},{8,9},{9,8},{10,11... | collective-permute-start | bytes 1474568 | tf_op jit(solution)/shard_map/ppermute | solution.py:234
  94.4 32.5 %collective-permute-start.18 = (bf16[160,1536]{1,0:T(8,128)(2,1)}, bf16[160,1536]{1,0:T(8,128)(2,1)}, u32[]{:S(2)}, u32[]{:S(2)}) collective-permute-start(bf16[160,1536]{1,0:T(8,128)(2,1)} %collective-permute-done.14.refs_1_), channel_id=1, source_target_pairs={{0,1},{1,0},{2,3},{3,2},{4,5},{5,4},{6,7},{7,6},{8,9},{9,8},{10,11... | collective-permute-start | bytes 1474568 | tf_op jit(solution)/shard_map/ppermute | solution.py:234
  94.9 32.6 %collective-permute-start.9 = (bf16[192,1536]{1,0:T(8,128)(2,1)S(1)}, bf16[192,1536]{1,0:T(8,128)(2,1)}, u32[]{:S(2)}, u32[]{:S(2)}) collective-permute-start(bf16[192,1536]{1,0:T(8,128)(2,1)S(1)} %collective-permute-done.7.refs_1_), channel_id=1, source_target_pairs={{0,2},{2,4},{4,6},{6,0},{1,3},{3,5},{5,7},{7,1},{8,10},{10,12},{12... | collective-permute-start | bytes 1769480 | tf_op jit(solution)/shard_map/ppermute | solution.py:234
  94.9 32.6 %collective-permute-start.20 = (bf16[160,1536]{1,0:T(8,128)(2,1)}, bf16[160,1536]{1,0:T(8,128)(2,1)}, u32[]{:S(2)}, u32[]{:S(2)}) collective-permute-start(bf16[160,1536]{1,0:T(8,128)(2,1)} %collective-permute-done.16.refs_3_), channel_id=1, source_target_pairs={{0,1},{1,0},{2,3},{3,2},{4,5},{5,4},{6,7},{7,6},{8,9},{9,8},{10,11... | collective-permute-start | bytes 1474568 | tf_op jit(solution)/shard_map/ppermute | solution.py:234
  122.3 33.0 %all-to-all-start.1 = ((bf16[8,192,128]{2,1,0:T(8,128)(2,1)}), bf16[8,192,128]{2,1,0:T(8,128)(2,1)}, u32[]{:S(2)}, u32[]{:S(2)}) async-start(bf16[8,192,128]{2,1,0:T(8,128)(2,1)} %copy-done.7), calls=%async_computation.1 | async-start | bytes 786432 | tf_op jit(solution)/shard_map/all_to_all | solution.py:304
  126.4 33.6 %collective-permute-start.10 = (bf16[192,1536]{1,0:T(8,128)(2,1)S(1)}, bf16[192,1536]{1,0:T(8,128)(2,1)}, u32[]{:S(2)}, u32[]{:S(2)}) collective-permute-start(bf16[192,1536]{1,0:T(8,128)(2,1)S(1)} %copy-done.2), channel_id=1, source_target_pairs={{0,1},{1,0},{2,3},{3,2},{4,5},{5,4},{6,7},{7,6},{8,9},{9,8},{10,11... | collective-permute-start | bytes 1769480 | tf_op jit(solution)/shard_map/ppermute | solution.py:234
  126.9 33.1 %collective-permute-start.11 = (bf16[192,1536]{1,0:T(8,128)(2,1)S(1)}, bf16[192,1536]{1,0:T(8,128)(2,1)}, u32[]{:S(2)}, u32[]{:S(2)}) collective-permute-start(bf16[192,1536]{1,0:T(8,128)(2,1)S(1)} %collective-permute-done.7.refs_1_), channel_id=1, source_target_pairs={{0,1},{1,0},{2,3},{3,2},{4,5},{5,4},{6,7},{7,6},{8,9},{9,8},{10,11... | collective-permute-start | bytes 1769480 | tf_op jit(solution)/shard_map/ppermute | solution.py:234
  127.0 33.0 %collective-permute-start.12 = (bf16[192,1536]{1,0:T(8,128)(2,1)S(1)}, bf16[192,1536]{1,0:T(8,128)(2,1)}, u32[]{:S(2)}, u32[]{:S(2)}) collective-permute-start(bf16[192,1536]{1,0:T(8,128)(2,1)S(1)} %collective-permute-done.8.refs_2_), channel_id=1, source_target_pairs={{0,1},{1,0},{2,3},{3,2},{4,5},{5,4},{6,7},{7,6},{8,9},{9,8},{10,11... | collective-permute-start | bytes 1769480 | tf_op jit(solution)/shard_map/ppermute | solution.py:234
  127.5 32.6 %collective-permute-start.13 = (bf16[192,1536]{1,0:T(8,128)(2,1)}, bf16[192,1536]{1,0:T(8,128)(2,1)}, u32[]{:S(2)}, u32[]{:S(2)}) collective-permute-start(bf16[192,1536]{1,0:T(8,128)(2,1)} %collective-permute-done.9.refs_3_), channel_id=1, source_target_pairs={{0,1},{1,0},{2,3},{3,2},{4,5},{5,4},{6,7},{7,6},{8,9},{9,8},{10,11... | collective-permute-start | bytes 1769480 | tf_op jit(solution)/shard_map/ppermute | solution.py:234
  186.5 17.3 %collective-permute-start.21 = (bf16[128,1536]{1,0:T(8,128)(2,1)}, bf16[128,1536]{1,0:T(8,128)(2,1)S(1)}, u32[]{:S(2)}, u32[]{:S(2)}) collective-permute-start(bf16[128,1536]{1,0:T(8,128)(2,1)} %get-tuple-element.12.refs_0_), channel_id=1, source_target_pairs={{0,1},{1,0},{2,3},{3,2},{4,5},{5,4},{6,7},{7,6},{8,9},{9,8},{10,11... | collective-permute-start | bytes 1179656 | tf_op jit(solution)/shard_map/ppermute | solution.py:234
  187.0 16.8 %collective-permute-start.22 = (bf16[128,1536]{1,0:T(8,128)(2,1)}, bf16[128,1536]{1,0:T(8,128)(2,1)S(1)}, u32[]{:S(2)}, u32[]{:S(2)}) collective-permute-start(bf16[128,1536]{1,0:T(8,128)(2,1)} %get-tuple-element.13.refs_1_), channel_id=1, source_target_pairs={{0,1},{1,0},{2,3},{3,2},{4,5},{5,4},{6,7},{7,6},{8,9},{9,8},{10,11... | collective-permute-start | bytes 1179656 | tf_op jit(solution)/shard_map/ppermute | solution.py:234
  216.3 20.0 %collective-permute-start.30 = (bf16[256,1536]{1,0:T(8,128)(2,1)S(1)}, bf16[256,1536]{1,0:T(8,128)(2,1)S(1)}, u32[]{:S(2)}, u32[]{:S(2)}) collective-permute-start(bf16[256,1536]{1,0:T(8,128)(2,1)S(1)} %add_convert_fusion), channel_id=1, source_target_pairs={{0,64},{64,0},{1,65},{65,1},{2,66},{66,2},{3,67},{67,3},{4,68},{68... | collective-permute-start | bytes 2359304 | tf_op jit(solution)/shard_map/ppermute | solution.py:234
  (41 other events, 360.4 us)
Sparse Core Ops, SparseCore 0:
  19.7 109.4 all-gather.1
